TPU v7x, 32 devices: a whole 2x2x4 slice. The times are simulated.
32 devices in a mesh: rcv: 4 (over y, core), slab: 8 (over z, x).
Axes of the slice: x: 2, y: 2, z: 4, core: 2. Of those that a mesh axis runs over, the one named last changes fastest.
Arguments:
- displacement: bfloat16 [2, 16, 3, 16, 16, 1024], P(None, None, None, 'slab'), may hold values from -6 to 6
- green: bfloat16 [8, 16, 6, 16, 16, 1024], P('rcv', None, None, 'slab'), may hold values from -0.1796875 to 0.1796875
- lame_lambda: float32 [16, 16, 1024], P('slab'), may hold values from 0.5 to 2
- shear_modulus: float32 [16, 16, 1024], P('slab'), may hold values from 0.3 to 1.5
- filters: float32 [2, 8, 9], P(None, 'rcv'), may hold values from -2 to 2
- pairs: int32 [2, 8], P(None, 'rcv'), may hold values 0 or 1
Outputs:
- kernels: float32 [2, 16, 16, 1024], P(None, 'slab', 'rcv')
Inputs may be any that keep to these rules, and one draw needn't show every extreme that they name: `pairs`: 1 marks a pair that is used, 0 one that is not.
All inputs are finite; a program needn't handle non-finite values. No bound on the sum of `pairs` on one device may be relied on, other than what follows from the above.
Results may differ from a plain program's by a relative error of at most 0.0029.
Values may be sent and summed in bfloat16 or wider, within the bound.
No kernel may reach another device: no remote copies, remote signals or barrier semaphores. Data moves between devices by JAX's collectives and lax.ppermute only.
A program may use at most 192 MiB of HBM per device.

v0:
```python
import jax
import jax.numpy as jnp
from jax import lax
from jax.sharding import PartitionSpec as P


def padded_2(array, sides, width):
    for axis, dim in sides:
        devices, length = (lax.axis_size(axis), array.shape[dim])
        up = [(i, (i + 1) % devices) for i in range(devices - 1)]
        down = [(j, i) for i, j in up]
        last = lax.slice_in_dim(array, length - width, length, axis=dim)
        initial = lax.slice_in_dim(array, 0, width, axis=dim)
        before = lax.ppermute(last, axis, up)
        after = lax.ppermute(initial, axis, down)
        array = jnp.concatenate([before, array, after], axis=dim)
    return array


def derivative(field, axis):
    length = field.shape[axis]
    pad_width = [(0, 0)] * field.ndim
    pad_width[axis] = (2, 2)
    padded = jnp.pad(field, pad_width)

    def window(offset):
        return lax.slice_in_dim(padded, 2 + offset, 2 + offset + length, axis=axis)

    return (8.0 * (window(1) - window(-1)) - (window(2) - window(-2))) / 12.0


def depth_derivative(extended, length):

    def window(offset):
        return lax.slice_in_dim(extended, 2 + offset, 2 + offset + length, axis=3)

    return (8.0 * (window(1) - window(-1)) - (window(2) - window(-2))) / 12.0


def compose(along_cols, along_rows, along_depth, lame_lambda, shear_modulus):
    strain_xx = along_cols[:, :, 0]
    strain_yy = along_rows[:, :, 1]
    strain_zz = along_depth[:, :, 2]
    strain_yz = 0.5 * (along_depth[:, :, 1] + along_rows[:, :, 2])
    strain_xz = 0.5 * (along_depth[:, :, 0] + along_cols[:, :, 2])
    strain_xy = 0.5 * (along_rows[:, :, 0] + along_cols[:, :, 1])
    strain_trace = strain_xx + strain_yy + strain_zz
    volume_term = lame_lambda * strain_trace
    double_shear = 2.0 * shear_modulus
    components = [
        volume_term + double_shear * strain_xx,
        volume_term + double_shear * strain_yy,
        volume_term + double_shear * strain_zz,
        double_shear * strain_yz,
        double_shear * strain_xz,
        double_shear * strain_xy,
    ]
    return jnp.stack(components, axis=2).astype(jnp.bfloat16)


def contribution(stress_one, filter_taps, green_one):
    lag_total = filter_taps.shape[0]
    half_lags = lag_total // 2
    snap_count = stress_one.shape[0]
    padded = jnp.pad(stress_one, [(half_lags, half_lags)] + [(0, 0)] * (stress_one.ndim - 1))
    filtered = jnp.zeros(stress_one.shape, jnp.float32)
    for lag_index in range(lag_total):
        filtered = filtered + filter_taps[lag_index] * padded[
            lag_index : lag_index + snap_count
        ].astype(jnp.float32)
    weights = jnp.array([1.0, 1.0, 1.0, 2.0, 2.0, 2.0], jnp.float32).reshape(1, 6, 1, 1, 1)
    return jnp.sum(filtered * green_one.astype(jnp.float32) * weights, axis=(0, 1))


def on_device(displacement, green, lame_lambda, shear_modulus, filters, pairs):
    sources, snap_count, components, planes, row_count, col_count = displacement.shape
    groups = lax.axis_size("rcv")
    member = lax.axis_index("rcv")
    flat = displacement.reshape((sources * snap_count, components, planes, row_count, col_count))
    share = flat.shape[0] // groups
    mine = lax.dynamic_slice_in_dim(flat, member * share, share, 0)
    grown = padded_2(mine, (("slab", 2),), 2)
    edges = jnp.concatenate([grown[:, :, 0:2], grown[:, :, planes + 2 : planes + 4]], axis=2)
    every_edge = lax.all_gather(edges, "rcv", axis=0, tiled=True)
    joined = jnp.concatenate([every_edge[:, :, 0:2], flat, every_edge[:, :, 2:4]], axis=2)
    extended = joined.reshape((sources, snap_count, components, planes + 4, row_count, col_count))
    field = extended.astype(jnp.float32)
    interior = field[:, :, :, 2 : planes + 2]
    along_depth = depth_derivative(field, planes)
    along_rows = derivative(interior, 4)
    along_cols = derivative(interior, 5)
    stress = compose(along_cols, along_rows, along_depth, lame_lambda, shear_modulus)
    station_count = green.shape[0]
    slots = sources * station_count
    flat_pairs = pairs.reshape(-1)
    initial = jnp.zeros((sources, planes, row_count, col_count), jnp.float32)

    def add_slot(slot, kernel_acc, weight):
        source = slot // station_count
        station = slot % station_count
        stress_one = lax.dynamic_index_in_dim(stress, source, 0, keepdims=False)
        green_one = lax.dynamic_index_in_dim(green, station, 0, keepdims=False)
        filter_taps = filters[source, station]
        term = weight * contribution(stress_one, filter_taps, green_one)
        current = lax.dynamic_index_in_dim(kernel_acc, source, 0, keepdims=False)
        return lax.dynamic_update_index_in_dim(kernel_acc, current + term, source, 0)

    def add_masked(slot, kernel_acc):
        return add_slot(slot, kernel_acc, flat_pairs[slot].astype(jnp.float32))

    kernel_acc = lax.fori_loop(0, slots, add_masked, initial)
    return lax.psum_scatter(kernel_acc, "rcv", scatter_dimension=2, tiled=True)


def solution(mesh):
    placed = (
        P(None, None, None, "slab", None, None),
        P("rcv", None, None, "slab", None, None),
        P("slab", None, None),
        P("slab", None, None),
        P(None, "rcv", None),
        P(None, "rcv"),
    )
    return jax.shard_map(
        on_device,
        mesh=mesh,
        in_specs=placed,
        out_specs=P(None, "slab", "rcv", None),
        check_vma=False,
    )
```

profile of v0, /device:TPU:0, one launch (start us, length us, event | category | flops | bytes accessed | tf_op | source)
XLA Modules:
  0.0 495.1 jit_solution(11546847999297486046)
XLA Ops:
  6.5 0.0 copy-start.5
  6.5 0.0 copy-start.2
  6.5 0.0 all-gather.2.cloned.1.call-start
  6.5 1.6 constant_dynamic-slice_fusion.2
  8.2 5.0 %collective-permute-start = (bf16[8,3,2,16,1024]{4,3,2,1,0:T(8,128)(2,1)S(1)}, bf16[8,3,2,16,1024]{4,3,2,1,0:T(8,128)(2,1)S(1)}, u32[]{:S(2)}, u32[]{:S(2)}) collective-permute-start(bf16[8,3,2,16,1024]{4,3,2,1,0:T(8,128)(2,1)S(1)} %constant_dynamic-slice_fusion.2), channel_id=1, source_target_pairs={{0,1},{1,2},{2,3},{3,4},{4,5},{5,6},{6,7},{8,9},{9,10},{10,11},{11... | collective-permute-start | bytes 4718600 | tf_op jit(solution)/shard_map/ppermute | solution.py:14
  13.1 1.3 collective-permute-start.1
  14.4 65.9 %collective-permute-done = bf16[8,3,2,16,1024]{4,3,2,1,0:T(8,128)(2,1)S(1)} collective-permute-done((bf16[8,3,2,16,1024]{4,3,2,1,0:T(8,128)(2,1)S(1)}, bf16[8,3,2,16,1024]{4,3,2,1,0:T(8,128)(2,1)S(1)}, u32[]{:S(2)}, u32[]{:S(2)}) %collective-permute-start) | collective-permute-done | bytes 1572896 | tf_op jit(solution)/shard_map/ppermute | solution.py:14
  80.4 0.0 collective-permute-done.1
  80.4 1.9 pad_maximum_fusion
  82.3 0.0 all-gather.2.cloned.1.call-update
  82.3 0.0 all-reduce.6.cloned.1.call-start
  82.4 0.0 copy-done.5
  82.4 0.1 reshape.52
  82.5 0.0 copy-done.2
  82.5 84.3 %all-gather.2.cloned.1.call-done = bf16[32,3,4,16,1024]{4,3,2,1,0:T(8,128)(2,1)} async-done(((bf16[8,3,4,16,1024]{4,3,2,1,0:T(8,128)(2,1)}), bf16[32,3,4,16,1024]{4,3,2,1,0:T(8,128)(2,1)}) %all-gather.2.cloned.1.call-update) | async-done | bytes 12582928 | tf_op jit(solution)/shard_map/all_gather | solution.py:84
  166.8 5.6 %fusion.29 = (bf16[32,3,2,16,1024]{4,3,2,1,0:T(8,128)(2,1)S(1)}, bf16[32,3,2,16,1024]{4,3,2,1,0:T(8,128)(2,1)S(1)}) fusion(bf16[32,3,4,16,1024]{4,3,2,1,0:T(8,128)(2,1)} %all-gather.2.cloned.1.call-done), kind=kLoop, calls=%fused_computation.63 | loop fusion | bytes 25165824 | tf_op jit(solution)/shard_map/slice | solution.py:85
  172.3 14.7 %maximum_convert_fusion = f32[2,16,3,6,16,1024]{5,4,3,2,1,0:T(8,128)} fusion(bf16[2,16,3,2,16,1024]{5,4,3,2,1,0:T(8,128)(2,1)S(1)} %bitcast.54, bf16[2,16,3,2,16,1024]{5,4,3,2,1,0:T(8,128)(2,1)} %param.9, bf16[2,16,3,2,16,1024]{5,4,3,2,1,0:T(8,128)(2,1)S(1)} %bitcast.53), kind=kLoop, calls=%fused_computation.19 | loop fusion | flops 28311552 | bytes 56623104 | tf_op jit(solution)/shard_map/convert_element_type | solution.py:87
  187.0 31.9 %fusion.14 = (f32[2,16,3,2,16,1024]{5,4,3,2,1,0:T(8,128)}, f32[2,16,3,2,16,1024]{5,4,3,2,1,0:T(8,128)}) fusion(f32[2,16,3,6,16,1024]{5,4,3,2,1,0:T(8,128)} %maximum_convert_fusion), kind=kLoop, calls=%fused_computation.36 | loop fusion | flops 15728640 | bytes 88080384 | tf_op jit(solution)/shard_map/div | solution.py:37
  218.9 43.1 %fusion.11 = (f32[2,16,3,2,16,1024]{5,4,3,2,1,0:T(8,128)}, f32[2,16,3,2,16,1024]{5,4,3,2,1,0:T(8,128)}) fusion(f32[2,16,3,2,16,1024]{5,4,3,2,1,0:T(8,128)} %get-tuple-element.231), kind=kLoop, calls=%fused_computation.32 | loop fusion | flops 31457280 | bytes 37748736 | tf_op jit(solution)/shard_map/div | solution.py:29
  262.0 0.0 copy-done.3
  262.0 6.4 %fusion.22 = (bf16[2,16,6,2,16,1024]{5,4,3,2,1,0:T(8,128)(2,1)S(1)}, f32[2,16,1,2,16,1024]{5,4,3,2,1,0:T(8,128)S(1)}) fusion(f32[2,16,3,2,16,1024]{5,4,3,2,1,0:T(8,128)} %get-tuple-element.233, f32[2,16,1024]{2,1,0:T(8,128)S(1)} %broadcast_multiply_fusion, f32[2,16,3,2,16,1024]{5,4,3,2,1,0:T(8,128)} %get-tuple-element.230, ...), kind=kLoop, calls=%fused_computation.53 | loop fusion | flops 6291455 | bytes 19136512
  268.4 0.0 slice-start
  268.4 3.5 fusion.23
  271.9 0.0 slice-start.1
  271.9 3.5 fusion.24
  275.3 0.0 slice-start.2
  275.4 4.7 fusion.25
  280.1 0.0 slice-done
  280.1 0.0 slice-done.1
  280.1 0.0 slice-done.2
  280.1 0.0 copy-start.4
  280.1 3.3 fusion.26
  283.5 3.3 fusion.27
  286.8 0.0 copy-start
  286.8 4.5 copy-done
  291.3 0.0 copy-done.4
  291.3 162.3 %while.16 = (s32[]{:T(128)}, f32[2,2,16,1024]{3,2,1,0:T(8,128)S(1)}, s32[4]{0:T(128)S(1)}, f32[2,2,9]{2,1,0:T(2,128)}, bf16[2,16,6,2,16,1024]{5,4,3,2,1,0:T(8,12...) while((s32[]{:T(128)}, ...), condition=%wide.region_2.3_spmd.clone, body=%wide.region_0.2_spmd.sunk.clone.sunk | while | flops 94404624 | bytes 25690652 | solution.py:111
  291.3 6.8 %dynamic-slice_bitcast_fusion.2 = bf16[16,6,2,16,1024]{4,3,2,1,0:T(8,128)(2,1)} fusion(bf16[2,16,6,2,16,1024]{5,4,3,2,1,0:T(8,128)(2,1)} %get-tuple-element.317, s32[]{:T(128)S(6)} %select_n.84), kind=kLoop, calls=%fused_computation.11.clone.1 | loop fusion | bytes 12582916 | tf_op jit(solution)/shard_map/while/body/eval_jaxpr/jit(dynamic_index_in_dim)/squeeze | solution.py:101
  298.1 0.7 constant_dynamic-slice_fusion.4
  298.8 0.7 fusion.33
  299.4 31.1 %fusion.34 = f32[2,16,1024]{2,1,0:T(8,128)S(1)} fusion(bf16[16,6,2,16,1024]{4,3,2,1,0:T(8,128)(2,1)} %dynamic-slice_bitcast_fusion.2, f32[6]{0:T(128)S(1)} %get-tuple-element.323, bf16[2,16,6,2,16,1024]{5,4,3,2,1,0:T(8,128)(2,1)} %get-tuple-element.318, s32[]{:T(128)S(6)} %select_n.86, f32[]{:T(128)} %bitcast.41, f32[]{:T(128)} %bitcast.42, ...), kind=kLoop, calls=%fused_computation.10.clone.1 | loop fusion | flops 94339072 | bytes 12714048 | tf_op jit(solution)/shard_map/while/body/eval_jaxpr/reduce_sum | solution.py:72
  330.6 0.6 dynamic_slice.80
  331.8 6.8 %dynamic-slice_bitcast_fusion.2 = bf16[16,6,2,16,1024]{4,3,2,1,0:T(8,128)(2,1)} fusion(bf16[2,16,6,2,16,1024]{5,4,3,2,1,0:T(8,128)(2,1)} %get-tuple-element.317, s32[]{:T(128)S(6)} %select_n.84), kind=kLoop, calls=%fused_computation.11.clone.1 | loop fusion | bytes 12582916 | tf_op jit(solution)/shard_map/while/body/eval_jaxpr/jit(dynamic_index_in_dim)/squeeze | solution.py:101
  338.6 0.7 constant_dynamic-slice_fusion.4
  339.3 0.7 fusion.33
  340.0 31.2 %fusion.34 = f32[2,16,1024]{2,1,0:T(8,128)S(1)} fusion(bf16[16,6,2,16,1024]{4,3,2,1,0:T(8,128)(2,1)} %dynamic-slice_bitcast_fusion.2, f32[6]{0:T(128)S(1)} %get-tuple-element.323, bf16[2,16,6,2,16,1024]{5,4,3,2,1,0:T(8,128)(2,1)} %get-tuple-element.318, s32[]{:T(128)S(6)} %select_n.86, f32[]{:T(128)} %bitcast.41, f32[]{:T(128)} %bitcast.42, ...), kind=kLoop, calls=%fused_computation.10.clone.1 | loop fusion | flops 94339072 | bytes 12714048 | tf_op jit(solution)/shard_map/while/body/eval_jaxpr/reduce_sum | solution.py:72
  371.2 0.6 dynamic_slice.80
  372.5 6.8 %dynamic-slice_bitcast_fusion.2 = bf16[16,6,2,16,1024]{4,3,2,1,0:T(8,128)(2,1)} fusion(bf16[2,16,6,2,16,1024]{5,4,3,2,1,0:T(8,128)(2,1)} %get-tuple-element.317, s32[]{:T(128)S(6)} %select_n.84), kind=kLoop, calls=%fused_computation.11.clone.1 | loop fusion | bytes 12582916 | tf_op jit(solution)/shard_map/while/body/eval_jaxpr/jit(dynamic_index_in_dim)/squeeze | solution.py:101
  379.2 0.7 constant_dynamic-slice_fusion.4
  379.9 0.7 fusion.33
  380.6 31.1 %fusion.34 = f32[2,16,1024]{2,1,0:T(8,128)S(1)} fusion(bf16[16,6,2,16,1024]{4,3,2,1,0:T(8,128)(2,1)} %dynamic-slice_bitcast_fusion.2, f32[6]{0:T(128)S(1)} %get-tuple-element.323, bf16[2,16,6,2,16,1024]{5,4,3,2,1,0:T(8,128)(2,1)} %get-tuple-element.318, s32[]{:T(128)S(6)} %select_n.86, f32[]{:T(128)} %bitcast.41, f32[]{:T(128)} %bitcast.42, ...), kind=kLoop, calls=%fused_computation.10.clone.1 | loop fusion | flops 94339072 | bytes 12714048 | tf_op jit(solution)/shard_map/while/body/eval_jaxpr/reduce_sum | solution.py:72
  411.7 0.6 dynamic_slice.80
  413.0 6.8 %dynamic-slice_bitcast_fusion.2 = bf16[16,6,2,16,1024]{4,3,2,1,0:T(8,128)(2,1)} fusion(bf16[2,16,6,2,16,1024]{5,4,3,2,1,0:T(8,128)(2,1)} %get-tuple-element.317, s32[]{:T(128)S(6)} %select_n.84), kind=kLoop, calls=%fused_computation.11.clone.1 | loop fusion | bytes 12582916 | tf_op jit(solution)/shard_map/while/body/eval_jaxpr/jit(dynamic_index_in_dim)/squeeze | solution.py:101
  419.8 0.7 constant_dynamic-slice_fusion.4
  420.4 0.7 fusion.33
  421.1 31.2 %fusion.34 = f32[2,16,1024]{2,1,0:T(8,128)S(1)} fusion(bf16[16,6,2,16,1024]{4,3,2,1,0:T(8,128)(2,1)} %dynamic-slice_bitcast_fusion.2, f32[6]{0:T(128)S(1)} %get-tuple-element.323, bf16[2,16,6,2,16,1024]{5,4,3,2,1,0:T(8,128)(2,1)} %get-tuple-element.318, s32[]{:T(128)S(6)} %select_n.86, f32[]{:T(128)} %bitcast.41, f32[]{:T(128)} %bitcast.42, ...), kind=kLoop, calls=%fused_computation.10.clone.1 | loop fusion | flops 94339072 | bytes 12714048 | tf_op jit(solution)/shard_map/while/body/eval_jaxpr/reduce_sum | solution.py:72
  452.3 0.6 dynamic_slice.80
  453.6 0.0 copy-start.1
  453.6 0.7 copy-done.1
  454.3 0.0 all-reduce.6.cloned.1.call-update
  454.3 0.0 copy-done.6
  454.3 0.6 dynamic-slice
  455.5 31.2 %all-reduce.6.cloned.1.call-done = f32[2,2,16,1024]{3,2,1,0:T(8,128)} async-done(((f32[2,2,16,1024]{3,2,1,0:T(8,128)}), f32[2,2,16,1024]{3,2,1,0:T(8,128)}) %all-reduce.6.cloned.1.call-update) | async-done | bytes 262160
  486.7 1.5 constant_dynamic-slice_fusion.1
  (9 shorter events, 0.1 us)
Async XLA Ops:
  6.5 75.8 %copy-start.5 = (s32[2,2]{1,0:T(2,128)S(1)}, s32[2,2]{1,0:T(2,128)}, u32[]{:S(2)}) copy-start(s32[2,2]{1,0:T(2,128)} %param.14) | copy-start | bytes 52
  6.5 75.9 %copy-start.2 = (f32[2,16,1024]{2,1,0:T(8,128)S(1)}, f32[2,16,1024]{2,1,0:T(8,128)}, u32[]{:S(2)}) copy-start(f32[2,16,1024]{2,1,0:T(8,128)} %param.12) | copy-start | bytes 393220
  6.5 160.2 %all-gather.2.cloned.1.call-start = ((), (), s32[]{:S(2)}) async-start(), calls=%async_computation | async-start | bytes 15728640 | tf_op jit(solution)/shard_map/all_gather | solution.py:84
  8.2 72.2 %collective-permute-start = (bf16[8,3,2,16,1024]{4,3,2,1,0:T(8,128)(2,1)S(1)}, bf16[8,3,2,16,1024]{4,3,2,1,0:T(8,128)(2,1)S(1)}, u32[]{:S(2)}, u32[]{:S(2)}) collective-permute-start(bf16[8,3,2,16,1024]{4,3,2,1,0:T(8,128)(2,1)S(1)} %constant_dynamic-slice_fusion.2), channel_id=1, source_target_pairs={{0,1},{1,2},{2,3},{3,4},{4,5},{5,6},{6,7},{8,9},{9,10},{10,11},{11... | collective-permute-start | bytes 4718600 | tf_op jit(solution)/shard_map/ppermute | solution.py:14
  13.1 67.2 %collective-permute-start.1 = (bf16[8,3,2,16,1024]{4,3,2,1,0:T(8,128)(2,1)S(1)}, bf16[8,3,2,16,1024]{4,3,2,1,0:T(8,128)(2,1)S(1)}, u32[]{:S(2)}, u32[]{:S(2)}) collective-permute-start(bf16[8,3,2,16,1024]{4,3,2,1,0:T(8,128)(2,1)S(1)} %constant_dynamic-slice_fusion.2), channel_id=1, source_target_pairs={{1,0},{2,1},{3,2},{4,3},{5,4},{6,5},{7,6},{9,8},{10,9},{11,10},{12... | collective-permute-start | bytes 4718600 | tf_op jit(solution)/shard_map/ppermute | solution.py:15
  82.3 404.4 %all-reduce.6.cloned.1.call-start = ((), (), s32[]{:S(2)}) async-start(), calls=%async_computation.1 | async-start | bytes 524288
  218.9 43.1 %copy-start.3 = (f32[2,16,1024]{2,1,0:T(8,128)S(1)}, f32[2,16,1024]{2,1,0:T(8,128)}, u32[]{:S(2)}) copy-start(f32[2,16,1024]{2,1,0:T(8,128)} %param.11) | copy-start | bytes 393220
  268.4 11.7 %slice-start = ((s8[12582912]{0:T(1024)(128)(4,1)}), s8[4194304]{0:T(1024)(128)(4,1)S(1)}, s32[]{:S(2)}) async-start(s8[12582912]{0:T(1024)(128)(4,1)} %bitcast.51), calls=%async_computation.2 | async-start | bytes 8388608
  271.9 8.2 %slice-start.1 = ((s8[12582912]{0:T(1024)(128)(4,1)}), s8[4194304]{0:T(1024)(128)(4,1)S(1)}, s32[]{:S(2)}) async-start(s8[12582912]{0:T(1024)(128)(4,1)} %bitcast.51), calls=%async_computation.3 | async-start | bytes 8388608
  275.3 4.8 slice-start.2
  280.1 11.2 %copy-start.4 = (f32[6]{0:T(128)S(1)}, f32[6]{0:T(128)}, u32[]{:S(2)}) copy-start(f32[6]{0:T(128)} %constant.131.clone..sunk.2) | copy-start | bytes 76
  286.8 4.5 copy-start
  291.3 163.0 %copy-start.6 = (u32[32]{0:T(128)S(1)}, u32[32]{0:T(128)}, u32[]{:S(2)}) copy-start(u32[32]{0:T(128)} %constant.146) | copy-start | bytes 388
  453.6 0.7 copy-start.1
Sparse Core Ops, SparseCore 0:
  82.4 84.2 all-gather.1
  454.4 32.2 all-reduce.5
where the time goes:
time: 496 us; the launch traced here: 495 us
  other arithmetic  241 us (49%)
  waiting for transfers between devices  181 us (36%)
  local copies, waits for them, and re-layouts  49.5 us (10%)
  between operations  14.2 us (3%)
  starting transfers between devices  6.31 us (1%)
    reduce_sum x4, other arithmetic, contribution(): jnp.sum(filtered * green_one.astype(jnp.float32) * weights, axis=(0, 1))  125 us
    all_gather x1, waiting for transfers between devices, on_device(): every_edge = lax.all_gather(edges, 'rcv', axis=0, tiled=True)  84.3 us
    ppermute x1, waiting for transfers between devices, padded_2(): before = lax.ppermute(last, axis, up)  65.9 us
    div x1, other arithmetic, derivative(): return (8.0 * (window(1) - window(-1)) - (window(2) - window(-2))) / 12.0  43.1 us
    div x1, other arithmetic, depth_derivative(): return (8.0 * (window(1) - window(-1)) - (window(2) - window(-2))) / 12.0  31.9 us
    unnamed x3, waiting for transfers between devices  31.2 us
    squeeze x4, local copies, waits for them, and re-layouts, add_slot(): stress_one = lax.dynamic_index_in_dim(stress, source, 0, keepdims=False)  27.1 us
    unnamed x6, other arithmetic  21.3 us
  transfers between devices with their start and end apart: 4, of which 3 were waited for; matrix products, arithmetic and copies ran while one was open for 0% of the time, Pallas kernels for 0%

commit v1 on v0

v1 whole, which is shorter than its diff:
```python
import functools
import jax
import jax.numpy as jnp
from jax import lax
from jax.experimental import pallas as pl
from jax.experimental.pallas import tpu as pltpu
from jax.sharding import PartitionSpec as P

LANES = 128
F32 = jnp.float32
BF16 = jnp.bfloat16
ANY = pl.BlockSpec(memory_space=pl.ANY)
SMEM = pl.BlockSpec(memory_space=pltpu.SMEM)
VMEM = pl.BlockSpec(memory_space=pltpu.VMEM)


def stencil(offset):
    return (
        jnp.where(offset == 1, 8.0, 0.0)
        + jnp.where(offset == -1, -8.0, 0.0)
        + jnp.where(offset == 2, -1.0, 0.0)
        + jnp.where(offset == -2, 1.0, 0.0)
    )


def iota(shape, axis):
    return lax.broadcasted_iota(jnp.int32, shape, axis)


def mm(a, b):
    return jnp.dot(a, b, preferred_element_type=F32)


def fill_tables(filters_ref, pairs_ref, mix_ref, dcol_ref, drow_ref, rows):
    sources, stations, lags = filters_ref.shape
    points = mix_ref.shape[0] // sources
    snaps = points // rows
    depth = mix_ref.shape[1]
    shape = (snaps, stations * snaps)
    station, at = iota(shape, 1) // snaps, iota(shape, 1) % snaps
    lag = iota(shape, 0) - at + lags // 2
    spread = (iota((points, snaps), 0) // rows == iota((points, snaps), 1)).astype(BF16)
    fan = (iota((depth // rows, depth), 1) // rows == iota((depth // rows, depth), 0)).astype(BF16)
    same = iota((points, depth), 0) % rows == iota((points, depth), 1) % rows
    for e in range(sources):
        table = jnp.zeros(shape, F32)
        for r in range(stations):
            used = pairs_ref[e, r].astype(F32)
            for j in range(lags):
                table = jnp.where((station == r) & (lag == j), used * filters_ref[e, r, j], table)
        high = table.astype(BF16)
        low = (table - high.astype(F32)).astype(BF16)
        taps = jnp.concatenate([high, low], axis=1)
        full = mm(mm(spread, taps).astype(BF16), fan)
        mix_ref[pl.ds(e * points, points)] = jnp.where(same, full, 0.0).astype(BF16)
    shape = dcol_ref.shape
    width = shape[1]
    place = iota(shape, 0)
    source = jnp.where(place < width, place, jnp.where(place < width + LANES, place - width - LANES, place - LANES))
    dcol_ref[...] = stencil(source - iota(shape, 1)).astype(BF16)
    shape = drow_ref.shape[1:]
    row, full = iota(shape, 0), iota(shape, 1)
    near = row // rows == full // (2 * rows)
    for h in range(2):
        drow_ref[h] = jnp.where(near, stencil(full % (2 * rows) - row % rows - h * rows), 0.0).astype(BF16)


def prepare(array, block, width, sizes, filters, pairs, snaps):
    tail = array.shape[1:-1] + (width,)
    starts = [sum(sizes[:k]) for k in range(len(sizes))]
    sources, stations, _ = filters.shape
    rows = array.shape[-2]
    points = snaps * rows // 2
    pieces = len(sizes)

    def kernel(block_ref, filters_ref, pairs_ref, src, *rest):
        outs, (mix_ref, dcol_ref, drow_ref, held, sems) = rest[:pieces], rest[pieces:]
        start = pl.multiple_of(block_ref[0] * width, width)
        spans = [pl.ds(at, size) for at, size in zip(starts, sizes)]
        gets = [
            pltpu.make_async_copy(src.at[span, ..., pl.ds(start, width)], held.at[span], sems.at[0, k])
            for k, span in enumerate(spans)
        ]
        puts = [pltpu.make_async_copy(held.at[span], outs[k], sems.at[1, k]) for k, span in enumerate(spans)]
        for get in gets:
            get.start()
        fill_tables(filters_ref, pairs_ref, mix_ref, dcol_ref, drow_ref, rows // 2)
        for get, put in zip(gets, puts):
            get.wait()
            put.start()
        for put in puts:
            put.wait()

    out = pl.pallas_call(
        kernel,
        out_shape=[jax.ShapeDtypeStruct((size,) + tail, array.dtype) for size in sizes]
        + [
            jax.ShapeDtypeStruct((sources * points, 2 * stations * points), BF16),
            jax.ShapeDtypeStruct((width + 2 * LANES, width), BF16),
            jax.ShapeDtypeStruct((2, points, 2 * points), BF16),
        ],
        in_specs=[SMEM, SMEM, SMEM, ANY],
        out_specs=[ANY] * pieces + [VMEM] * 3,
        scratch_shapes=[pltpu.VMEM(array.shape[:1] + tail, array.dtype), pltpu.SemaphoreType.DMA((2, pieces))],
        name="prepare",
    )(block.reshape(1), filters, pairs, array)
    return out[:pieces], out[pieces:]


def local_kernel(
    block_ref, mix_ref, dcol_ref, drow_ref, green_ref, left_ref, mid_ref, right_ref, lam_ref, mu_ref,
    *rest, last_block, waits, more,
):
    added = rest[waits : waits + more]
    part_ref, z_ref, gs, xs, ys = rest[waits + more :]
    snaps = z_ref.shape[2]
    rows, width = z_ref.shape[-2:]
    stations = green_ref.shape[0]
    half = rows // 2
    points = snaps * half
    span = lambda h: pl.ds(h * half, half)

    def filtered(*accs):
        k = 0
        for h in range(2):
            for c in range(0, 6, 2):
                for unit in range(2):
                    tile = green_ref[:, :, c + unit, 0, span(h)].reshape(stations * points, width)
                    pltpu.matmul_push_rhs(tile, staging_register=k % 2, mxu_index=unit)
                for part in range(2):
                    lhs = mix_ref[:, pl.ds(part * stations * points, stations * points)]
                    for unit in range(2):
                        acc = accs[2 * unit + k % 2]
                        pltpu.matmul_acc_lhs(acc, lhs, load_staged_rhs=k % 2 if part == 0 else None)
                for unit in range(2):
                    gs[c + unit, h] = pltpu.matmul_pop(accs[2 * unit + k % 2])
                k += 1

    block = block_ref[0]
    whole, ends = [], []
    for i in range(3):
        whole.append(mid_ref[0, :, i, 0].reshape(2 * points, width))
        left = left_ref[0, :, i, 0]
        right = right_ref[0, :, i, 0]
        left = jnp.where(block == 0, jnp.zeros_like(left), left)
        right = jnp.where(block == last_block, jnp.zeros_like(right), right)
        ends.append(jnp.concatenate([left, right], axis=2).reshape(2 * points, width))

    def columns(*accs):
        for tile, lhs in enumerate((whole, ends)):
            for unit in range(2):
                pltpu.matmul_push_rhs(dcol_ref[pl.ds(tile * width, width)], staging_register=tile, mxu_index=unit)
            for unit in range(2):
                pltpu.matmul_acc_lhs(accs[2 * unit], lhs[unit], load_staged_rhs=tile)
                pltpu.matmul_acc_lhs(accs[2 * unit + 1], lhs[2][unit * points : (unit + 1) * points])
        for unit in range(2):
            xs[unit] = pltpu.matmul_pop(accs[2 * unit])
            xs[2, pl.ds(unit * points, points)] = pltpu.matmul_pop(accs[2 * unit + 1])

    def lines(*accs):
        for unit in range(2):
            pltpu.matmul_push_rhs(whole[unit], staging_register=0, mxu_index=unit)
            pltpu.matmul_push_rhs(whole[2], staging_register=1, mxu_index=unit)
        for unit in range(2):
            pltpu.matmul_acc_lhs(accs[3 * unit], drow_ref[0], load_staged_rhs=0)
            pltpu.matmul_acc_lhs(accs[3 * unit + 1], drow_ref[1])
            pltpu.matmul_acc_lhs(accs[3 * unit + 2], drow_ref[unit], load_staged_rhs=1)
        for unit in range(2):
            ys[unit, 0] = pltpu.matmul_pop(accs[3 * unit])
            ys[unit, 1] = pltpu.matmul_pop(accs[3 * unit + 1])
            ys[2, unit] = pltpu.matmul_pop(accs[3 * unit + 2])

    space = lambda unit, size: pltpu.ACC(unit)((size, width), F32)
    pl.run_scoped(filtered, *[space(unit, points) for unit in range(2) for _ in range(2)])
    pl.run_scoped(columns, *[space(unit, size) for unit in range(2) for size in (2 * points, points)])
    pl.run_scoped(lines, *[space(unit, points) for unit in range(2) for _ in range(3)])

    zero = jnp.zeros((half, width), F32)
    for h in range(2):
        lam = lam_ref[0, span(h)]
        mu2 = 2.0 * mu_ref[0, span(h)]

        def step(s, carry):
            vol, dev = carry
            at = pl.ds(pl.multiple_of(s * half, half), half)
            full = pl.ds(pl.multiple_of((2 * s + h) * half, half), half)
            gxx, gyy, gzz, gyz, gxz, gxy = (gs[c, h, at] for c in range(6))
            gtr = gxx + gyy + gzz
            dxx, dyy = xs[0, full], ys[1, h, at]
            vol = vol + (dxx + dyy) * gtr
            dev = dev + (dxx * gxx + dyy * gyy) + (ys[2, h, at] * gyz + xs[2, full] * gxz)
            dev = dev + (xs[1, full] + ys[0, h, at]) * gxy
            for i, z in enumerate((mu2 * gxz, mu2 * gyz, lam * gtr + mu2 * gzz)):
                for ref in added:
                    z = z + ref[0, i, s, 0, span(h)].astype(F32)
                z_ref[0, i, s, 0, span(h)] = z.astype(BF16)
            return vol, dev

        vol, dev = lax.fori_loop(0, snaps, step, (zero, zero), unroll=4)
        part_ref[0, 0, span(h)] = (lam * vol + mu2 * dev) / 12.0


def local_terms(block, first, count, mats, green, displacement, lam, mu, width, after=(), add=()):
    _, snaps, _, planes, rows, cols = displacement.shape
    stations = green.shape[0]
    points = snaps * rows
    per = width // LANES
    top = cols // LANES - 1
    mix, dcol, drow = mats
    g_at = lambda e, z, b: (0, 0, 0, z, 0, b[0])
    u_at = lambda f: (lambda e, z, b: (first + e, 0, 0, z, 0, f(b[0])))
    m_at = lambda e, z, b: (z, 0, b[0])
    z_spec = pl.BlockSpec((1, 3, snaps, 1, rows, width), lambda e, z, b: (e, 0, 0, z, 0, 0))
    return pl.pallas_call(
        functools.partial(local_kernel, last_block=cols // width - 1, waits=len(after), more=len(add)),
        out_shape=(
            jax.ShapeDtypeStruct((count, planes, rows, width), F32),
            jax.ShapeDtypeStruct((count, 3, snaps, planes, rows, width), BF16),
        ),
        grid_spec=pltpu.PrefetchScalarGridSpec(
            num_scalar_prefetch=1,
            grid=(count, planes),
            in_specs=[
                pl.BlockSpec((points // 2, mix.shape[1]), lambda e, z, b: (first + e, 0)),
                pl.BlockSpec(dcol.shape, lambda e, z, b: (0, 0)),
                pl.BlockSpec(drow.shape, lambda e, z, b: (0, 0, 0)),
                pl.BlockSpec((stations, snaps, 6, 1, rows, width), g_at),
                pl.BlockSpec((1, snaps, 3, 1, rows, LANES), u_at(lambda b: jnp.maximum(per * b - 1, 0))),
                pl.BlockSpec((1, snaps, 3, 1, rows, width), u_at(lambda b: b)),
                pl.BlockSpec((1, snaps, 3, 1, rows, LANES), u_at(lambda b: jnp.minimum(per * b + per, top))),
                pl.BlockSpec((1, rows, width), m_at),
                pl.BlockSpec((1, rows, width), m_at),
            ]
            + [ANY] * len(after)
            + [z_spec] * len(add),
            out_specs=(pl.BlockSpec((1, 1, rows, width), lambda e, z, b: (e, z, 0, 0)), z_spec),
            scratch_shapes=[
                pltpu.VMEM((6, 2, points // 2, width), F32),
                pltpu.VMEM((3, points, width), F32),
                pltpu.VMEM((3, 2, points // 2, width), F32),
            ],
        ),
        cost_estimate=pl.CostEstimate(
            flops=int(count * planes * 2 * width * points * (6 * stations * points + 3 * 2 * width + 3 * points)),
            bytes_accessed=int(count * planes * width * rows * snaps * (6 * stations + 9) * 2),
            transcendentals=0,
        ),
        name="local_terms",
    )(block.reshape(1), mix, dcol, drow, green, displacement, displacement, displacement, lam, mu, *after, *add)


def depth_kernel(coef_ref, own_ref, near_ref, far_ref, z0_ref, z1_ref, old_ref, new_ref):
    snaps = own_ref.shape[0]

    def step(s, carry):
        top, bottom = carry
        for i in range(3):
            own0, own1 = own_ref[s, i, 0].astype(F32), own_ref[s, i, 1].astype(F32)
            n0, n1 = near_ref[s, i, 0].astype(F32), near_ref[s, i, 1].astype(F32)
            f0, f1 = far_ref[s, i, 0].astype(F32), far_ref[s, i, 1].astype(F32)
            d0 = 8.0 * own1 + (coef_ref[0] * n0 + coef_ref[1] * n1) + (coef_ref[2] * f0 + coef_ref[3] * f1)
            d1 = (coef_ref[4] * n0 + coef_ref[5] * n1) + (coef_ref[6] * f0 + coef_ref[7] * f1) - 8.0 * own0
            z = [z0_ref[0, i, s, p].astype(F32) + z1_ref[0, i, s, p].astype(F32) for p in range(2)]
            top = top + z[0] * d0
            bottom = bottom + z[1] * d1
        return top, bottom

    zero = jnp.zeros(new_ref.shape[1:], F32)
    top, bottom = lax.fori_loop(0, snaps, step, (zero, zero), unroll=2)

    @pl.when(pl.program_id(0) == 0)
    def _():
        new_ref[...] = old_ref[...]

    new_ref[0] += top / 12.0
    new_ref[1] += bottom / 12.0


def depth_terms(coefs, own, near, far, z0, z1, old, source, at, lead, count, unit):
    comps, planes, rows, width = own.shape[1:]
    whole = pl.BlockSpec(old.shape, lambda s: (0,) * old.ndim)
    u_spec = pl.BlockSpec((unit,) + own.shape[1:], lambda s: (lead // unit + s, 0, 0, 0, 0))
    z_spec = lambda e: pl.BlockSpec((1, comps, unit, planes, rows, width), lambda s: (e, 0, at // unit + s, 0, 0, 0))
    return pl.pallas_call(
        depth_kernel,
        out_shape=jax.ShapeDtypeStruct((planes, rows, width), F32),
        grid=(count // unit,),
        in_specs=[SMEM] + [u_spec] * 3 + [z_spec(source), z_spec(0), whole],
        out_specs=whole,
        name="depth_terms",
    )(coefs, own, near, far, z0, z1, old)


def cut_kernel(me_ref, *refs, groups):
    total, outs, held = refs[: -groups - 1], refs[-groups - 1 : -1], refs[-1]
    part = outs[0].shape[2]
    for q in range(groups):
        for e, ref in enumerate(total):
            held[q, e] = ref[:, q * part : (q + 1) * part, :]
    for bits, out in enumerate(outs):
        out[...] = held[me_ref[0] ^ bits]


def cut_rows(me, totals, groups):
    planes, rows, width = totals[0].shape
    shape = (len(totals), planes, rows // groups, width)
    return pl.pallas_call(
        functools.partial(cut_kernel, groups=groups),
        out_shape=[jax.ShapeDtypeStruct(shape, F32)] * groups,
        in_specs=[SMEM] + [VMEM] * len(totals),
        out_specs=[VMEM] * groups,
        scratch_shapes=[pltpu.VMEM((groups,) + shape, F32)],
        name="cut_rows",
    )(me.reshape(1), *totals)


def spread_kernel(me_ref, *refs, groups, counts):
    ins, outs, held = refs[: -groups - 1], refs[-groups - 1 : -1], refs[-1]
    part = outs[0].shape[2]
    at = 0
    for bits, count in enumerate(counts):
        e = 0
        for ref in ins[at : at + count]:
            width = ref.shape[-1]
            columns = pl.ds(pl.multiple_of((me_ref[0] ^ bits) * width, width), width)
            for k in range(ref.shape[0]):
                for q in range(groups):
                    held[q, e, :, :, columns] = ref[k, :, q * part : (q + 1) * part, :]
                e += 1
        at += count
    for bits, out in enumerate(outs):
        out[...] = held[me_ref[0] ^ bits]


def spread_rows(me, blocks, groups):
    planes, rows, width = blocks[0][0].shape[1:]
    sources = sum(piece.shape[0] for piece in blocks[0])
    shape = (sources, planes, rows // groups, width * len(blocks))
    flat = [piece for pieces in blocks for piece in pieces]
    return pl.pallas_call(
        functools.partial(spread_kernel, groups=groups, counts=[len(pieces) for pieces in blocks]),
        out_shape=[jax.ShapeDtypeStruct(shape, F32)] * groups,
        in_specs=[SMEM] + [VMEM] * len(flat),
        out_specs=[VMEM] * groups,
        scratch_shapes=[pltpu.VMEM((groups,) + shape, F32)],
        name="spread_rows",
    )(me.reshape(1), *flat)


def join_kernel(me_ref, base_ref, *refs):
    pieces, out = refs[:-1], refs[-1]
    width = pieces[0].shape[-1]
    for bits, piece in enumerate(pieces):
        columns = pl.ds(pl.multiple_of((me_ref[0] ^ bits) * width, width), width)
        out[..., columns] = base_ref[..., columns] + piece[...]


def join_columns(me, base, pieces):
    return pl.pallas_call(
        join_kernel,
        out_shape=jax.ShapeDtypeStruct(base.shape, F32),
        in_specs=[SMEM] + [VMEM] * (len(pieces) + 1),
        out_specs=VMEM,
        name="join_columns",
    )(me.reshape(1), base, *pieces)


SHARES = (1, 2, 2, 2, 1)


def on_device(displacement, green, lame_lambda, shear_modulus, filters, pairs):
    sources, snaps, _, planes, rows, cols = displacement.shape
    groups = lax.axis_size("rcv")
    slabs = lax.axis_size("slab")
    me = lax.axis_index("rcv")
    slab = lax.axis_index("slab")
    width = cols // groups
    pair_swap = [(i, i ^ 1) for i in range(slabs)]
    onward = [(i, i + 2 if i % 2 == 0 else i - 2) for i in range(slabs)]
    onward = [(i, j) for i, j in onward if 0 <= j < slabs]

    def swap(x, bit):
        return lax.ppermute(x, "rcv", [(i, i ^ bit) for i in range(groups)])

    def along(x, links):
        return lax.ppermute(x, "slab", links)

    def terms(bits, first, count, after=(), add=()):
        return local_terms(
            me ^ bits, first, count, mats, green, displacement, lame_lambda, shear_modulus, width, after, add
        )

    total_snaps = sources * snaps
    unit = total_snaps // sum(SHARES)
    sizes = [share * unit for share in SHARES]
    lead = displacement.reshape((total_snaps,) + displacement.shape[2:])
    own, mats = prepare(lead, me, width, sizes, filters, pairs, snaps)
    near = [along(piece, pair_swap) for piece in own]
    far = [along(piece, onward) for piece in near]

    across, parts = [], [[] for _ in range(groups)]
    last = own[0]
    sent = []
    for e in range(sources):
        part, last = terms(3, e, 1, (last,))
        parts[3].append(part)
        sent.append(swap(last, 1))
    for e in range(sources):
        part, last = terms(2, e, 1, (last,), (sent[e],))
        parts[2].append(part)
        across.append(swap(last, 2))
    part, last = terms(1, 0, sources, (last,))
    parts[1].append(part)
    part, z0 = terms(0, 0, sources, (last,), (swap(last, 1),))
    parts[0].append(part)
    base = spread_rows(me, parts, groups)
    base = sum([base[0]] + [swap(base[bits], bits) for bits in range(1, groups)])

    even = slab % 2 == 0
    coefs = jnp.where(
        even,
        jnp.array([-1, 0, 1, -8, 8, -1, 0, 1], F32),
        jnp.array([1, -8, -1, 0, 0, 1, 8, -1], F32),
    )
    totals = [jnp.zeros((planes, rows, width), F32)] * sources
    begin = 0
    for k, size in enumerate(sizes):
        at = begin
        while at < begin + size:
            e = at // snaps
            count = min(begin + size, (e + 1) * snaps) - at
            totals[e] = depth_terms(
                coefs, own[k], near[k], far[k], z0, across[e], totals[e], e, at % snaps, at - begin, count, unit
            )
            at += count
        begin += size
    pieces = cut_rows(me, totals, groups)
    pieces = [piece if bits == 0 else swap(piece, bits) for bits, piece in enumerate(pieces)]
    return join_columns(me, base, pieces)


def solution(mesh):
    placed = (
        P(None, None, None, "slab", None, None),
        P("rcv", None, None, "slab", None, None),
        P("slab", None, None),
        P("slab", None, None),
        P(None, "rcv", None),
        P(None, "rcv"),
    )
    return jax.shard_map(
        on_device,
        mesh=mesh,
        in_specs=placed,
        out_specs=P(None, "slab", "rcv", None),
        check_vma=False,
    )
```

time: 496 us -> 128 us (0.26)
  other arithmetic: 241 us -> 1.19 us
  waiting for transfers between devices: 181 us -> 29 us
  Pallas kernels: 0 us -> 61.1 us
  local copies, waits for them, and re-layouts: 49.5 us -> 3.74 us
  starting transfers between devices: 6.31 us -> 31.6 us
  between operations: 14.2 us -> 0.2 us
    reduce_sum x4 -> x0, other arithmetic: 125 us -> none  [contribution(): jnp.sum(filtered * green_one.astype(jnp.float32) * weights, axis=(0, 1))]
    all_gather x1 -> x0, waiting for transfers between devices: 84.3 us -> none  [on_device(): every_edge = lax.all_gather(edges, 'rcv', axis=0, tiled=True)]
    div x2 -> x0, other arithmetic: 75 us -> none  [the longest x1 43.1 us: derivative(): return (8.0 * (window(1) - window(-1)) - (window(2) - window(-2))) / 12.0]
    pallas_call x0 -> x16, Pallas kernels: none -> 61.1 us  [the longest x6 39.1 us: local_terms(): pl.pallas_call(functools.partial(local_kernel, last_block=cols // width -...]
    ppermute x2 -> x21, waiting for transfers between devices: 65.9 us -> 29 us  [the longest x10 25.2 us: along(): return lax.ppermute(x, 'slab', links)]
    unnamed x3 -> x0, waiting for transfers between devices: 31.2 us -> none
    squeeze x4 -> x0, local copies, waits for them, and re-layouts: 27.1 us -> none  [add_slot(): stress_one = lax.dynamic_index_in_dim(stress, source, 0, keepdims=False)]
    ppermute x2 -> x21, starting transfers between devices: 6.26 us -> 31.6 us  [the longest x10 24.9 us: along(): return lax.ppermute(x, 'slab', links)]
  transfers between devices with their start and end apart: 4 -> 21, of which waited for: 3 -> 6; matrix products, arithmetic and copies ran while one was open for 0% -> 1% of each run, Pallas kernels for 0% -> 29%
where the time goes in v1:
time: 128 us; the launch traced here: 127 us
  Pallas kernels  61.1 us (48%)
  starting transfers between devices  31.6 us (25%)
  waiting for transfers between devices  29 us (23%)
  local copies, waits for them, and re-layouts  3.74 us (3%)
    pallas_call x6, Pallas kernels, local_terms(): pl.pallas_call(functools.partial(local_kernel, last_block=cols // width -...  39.1 us
    ppermute x10, waiting for transfers between devices, along(): return lax.ppermute(x, 'slab', links)  25.2 us
    ppermute x10, starting transfers between devices, along(): return lax.ppermute(x, 'slab', links)  24.9 us
    pallas_call x6, Pallas kernels, depth_terms(): pl.pallas_call(depth_kernel, out_shape=jax.ShapeDtypeStruct((planes, rows...  13.4 us
    ppermute x11, starting transfers between devices, swap(): return lax.ppermute(x, 'rcv', [(i, i ^ bit) for i in range(groups)])  6.73 us
    pallas_call x1, Pallas kernels, prepare(): pl.pallas_call(kernel, out_shape=[jax.ShapeDtypeStruct((size,) + tail, ar...  4.02 us
    ppermute x11, waiting for transfers between devices, swap(): return lax.ppermute(x, 'rcv', [(i, i ^ bit) for i in range(groups)])  3.78 us
    unnamed x40, local copies, waits for them, and re-layouts  3.12 us
  transfers between devices with their start and end apart: 21, of which 6 were waited for; matrix products, arithmetic and copies ran while one was open for 1% of the time, Pallas kernels for 29%

profile of v1, /device:TPU:0, one launch (start us, length us, event | category | flops | bytes accessed | tf_op | source)
XLA Modules:
  0.0 126.8 jit_solution(12014555698200349782)
XLA Ops:
  0.0 4.0 %prepare.1 = (bf16[4,3,2,16,256]{4,3,2,1,0:T(8,128)(2,1)}, bf16[8,3,2,16,256]{4,3,2,1,0:T(8,128)(2,1)}, bf16[8,3,2,16,256]{4,3,2,1,0:T(8,128)(2,1)}, bf16[8,3,2,...) custom-call(s32[1]{0:T(128)} %bitcast.block_ref.me_ref, ...), custom_call_target="tpu_custom_call" | custom-call | tf_op jit(solution)/shard_map/prepare/pallas_call | solution.py:94
  4.0 5.3 %local_terms.6 = (f32[1,2,16,256]{3,2,1,0:T(8,128)}, bf16[1,3,16,2,16,256]{5,4,3,2,1,0:T(8,128)(2,1)}) custom-call(s32[1]{0:T(128)} %bitcast.4.block_ref, bf16[256,512]{1,0:T(8,128)(2,1)} %get-tuple-element.33.mix_ref, bf16[512,256]{1,0:T(8,128)(2,1)} %get-tuple-element.34.dcol_ref, bf16[2,128,256]{2,1,0:T(8,128)(2,1)} %get-tuple-element.35.drow_ref, ...), custom_call_target="tpu_custom_call" | custom-call | flops 1409286144 | bytes 5505024 | tf_op jit(solution)/shard_map/local_terms/pallas_call | solution.py:214
  9.3 0.5 collective-permute-start
  9.8 5.3 %local_terms.7 = (f32[1,2,16,256]{3,2,1,0:T(8,128)}, bf16[1,3,16,2,16,256]{5,4,3,2,1,0:T(8,128)(2,1)}) custom-call(s32[1]{0:T(128)} %bitcast.4.block_ref, bf16[256,512]{1,0:T(8,128)(2,1)} %get-tuple-element.33.mix_ref, bf16[512,256]{1,0:T(8,128)(2,1)} %get-tuple-element.34.dcol_ref, bf16[2,128,256]{2,1,0:T(8,128)(2,1)} %get-tuple-element.35.drow_ref, ...), custom_call_target="tpu_custom_call" | custom-call | flops 1409286144 | bytes 5505024 | tf_op jit(solution)/shard_map/local_terms/pallas_call | solution.py:214
  15.1 0.1 collective-permute-start.1
  15.2 0.0 collective-permute-done.rest_1_
  15.2 0.9 copy-done.6
  16.1 5.5 %local_terms.8 = (f32[1,2,16,256]{3,2,1,0:T(8,128)}, bf16[1,3,16,2,16,256]{5,4,3,2,1,0:T(8,128)(2,1)}) custom-call(s32[1]{0:T(128)} %bitcast.3.block_ref, bf16[256,512]{1,0:T(8,128)(2,1)} %get-tuple-element.33.mix_ref, bf16[512,256]{1,0:T(8,128)(2,1)} %get-tuple-element.34.dcol_ref, bf16[2,128,256]{2,1,0:T(8,128)(2,1)} %get-tuple-element.35.drow_ref, ...), custom_call_target="tpu_custom_call" | custom-call | flops 1409286144 | bytes 5505024 | tf_op jit(solution)/shard_map/local_terms/pallas_call | solution.py:214
  21.5 0.0 collective-permute-done.1.rest_1_
  21.6 0.9 copy-done.7
  22.4 5.5 %local_terms.9 = (f32[1,2,16,256]{3,2,1,0:T(8,128)}, bf16[1,3,16,2,16,256]{5,4,3,2,1,0:T(8,128)(2,1)}) custom-call(s32[1]{0:T(128)} %bitcast.3.block_ref, bf16[256,512]{1,0:T(8,128)(2,1)} %get-tuple-element.33.mix_ref, bf16[512,256]{1,0:T(8,128)(2,1)} %get-tuple-element.34.dcol_ref, bf16[2,128,256]{2,1,0:T(8,128)(2,1)} %get-tuple-element.35.drow_ref, ...), custom_call_target="tpu_custom_call" | custom-call | flops 1409286144 | bytes 5505024 | tf_op jit(solution)/shard_map/local_terms/pallas_call | solution.py:214
  27.9 8.6 %local_terms.10 = (f32[2,2,16,256]{3,2,1,0:T(8,128)}, bf16[2,3,16,2,16,256]{5,4,3,2,1,0:T(8,128)(2,1)}) custom-call(s32[1]{0:T(128)} %bitcast.2.block_ref, bf16[256,512]{1,0:T(8,128)(2,1)} %get-tuple-element.33.mix_ref, bf16[512,256]{1,0:T(8,128)(2,1)} %get-tuple-element.34.dcol_ref, bf16[2,128,256]{2,1,0:T(8,128)(2,1)} %get-tuple-element.35.drow_ref, ...), custom_call_target="tpu_custom_call" | custom-call | flops 2818572288 | bytes 11010048 | tf_op jit(solution)/shard_map/local_terms/pallas_call | solution.py:214
  36.6 0.4 collective-permute-start.2
  37.0 2.6 %collective-permute-start.6 = (bf16[8,3,2,16,256]{4,3,2,1,0:T(8,128)(2,1)S(1)}, bf16[8,3,2,16,256]{4,3,2,1,0:T(8,128)(2,1)}, u32[]{:S(2)}, u32[]{:S(2)}) collective-permute-start(bf16[8,3,2,16,256]{4,3,2,1,0:T(8,128)(2,1)S(1)} %copy-done.3), channel_id=1, source_target_pairs={{0,1},{1,0},{2,3},{3,2},{4,5},{5,4},{6,7},{7,6},{8,9},{9,8},{10,11... | collective-permute-start | bytes 1179656 | tf_op jit(solution)/shard_map/ppermute | solution.py:386
  39.6 0.1 collective-permute-start.16
  39.7 1.9 %collective-permute-start.13 = (bf16[4,3,2,16,256]{4,3,2,1,0:T(8,128)(2,1)S(1)}, bf16[4,3,2,16,256]{4,3,2,1,0:T(8,128)(2,1)S(1)}, u32[]{:S(2)}, u32[]{:S(2)}) collective-permute-start(bf16[4,3,2,16,256]{4,3,2,1,0:T(8,128)(2,1)S(1)} %copy-done.10), channel_id=1, source_target_pairs={{0,1},{1,0},{2,3},{3,2},{4,5},{5,4},{6,7},{7,6},{8,9},{9,8},{10,11... | collective-permute-start | bytes 589832 | tf_op jit(solution)/shard_map/ppermute | solution.py:386
  41.6 0.1 collective-permute-start.11
  41.7 20.5 %collective-permute-done.13.near_ref = bf16[4,3,2,16,256]{4,3,2,1,0:T(8,128)(2,1)S(1)} collective-permute-done((bf16[4,3,2,16,256]{4,3,2,1,0:T(8,128)(2,1)S(1)}, bf16[4,3,2,16,256]{4,3,2,1,0:T(8,128)(2,1)S(1)}, u32[]{:S(2)}, u32[]{:S(2)}) %collective-permute-start.13) | collective-permute-done | bytes 196640 | tf_op jit(solution)/shard_map/ppermute | solution.py:386
  62.2 2.0 %collective-permute-start.9 = (bf16[8,3,2,16,256]{4,3,2,1,0:T(8,128)(2,1)}, bf16[8,3,2,16,256]{4,3,2,1,0:T(8,128)(2,1)}, u32[]{:S(2)}, u32[]{:S(2)}) collective-permute-start(bf16[8,3,2,16,256]{4,3,2,1,0:T(8,128)(2,1)} %get-tuple-element.54.own_ref), channel_id=1, source_target_pairs={{0,1},{1,0},{2,3},{3,2},{4,5},{5,4},{6,7},{7,6},{8,9},{9,8},{10,11... | collective-permute-start | bytes 1179656 | tf_op jit(solution)/shard_map/ppermute | solution.py:386
  64.2 2.2 %collective-permute-done.11.near_ref = bf16[4,3,2,16,256]{4,3,2,1,0:T(8,128)(2,1)S(1)} collective-permute-done((bf16[4,3,2,16,256]{4,3,2,1,0:T(8,128)(2,1)S(1)}, bf16[4,3,2,16,256]{4,3,2,1,0:T(8,128)(2,1)S(1)}, u32[]{:S(2)}, u32[]{:S(2)}) %collective-permute-start.11) | collective-permute-done | bytes 196640 | tf_op jit(solution)/shard_map/ppermute | solution.py:386
  66.4 2.0 %collective-permute-start.15 = (bf16[1,3,16,2,16,256]{5,4,3,2,1,0:T(8,128)(2,1)}, bf16[1,3,16,2,16,256]{5,4,3,2,1,0:T(8,128)(2,1)S(1)}, u32[]{:S(2)}, u32[]{:S(2)}) collective-permute-start(bf16[1,3,16,2,16,256]{5,4,3,2,1,0:T(8,128)(2,1)} %get-tuple-element.40.rest_0_), channel_id=1, source_target_pairs={{0,16},{8,24},{16,0},{24,8},{1,17},{9,25},{17,1},{25,9},{2,18},{10... | collective-permute-start | bytes 2359304 | tf_op jit(solution)/shard_map/ppermute | solution.py:383
  68.4 0.0 collective-permute-done.6.near_ref
  68.4 0.1 collective-permute-start.8
  68.5 0.0 collective-permute-done.16.near_ref
  68.5 4.6 %collective-permute-start.12 = (bf16[4,3,2,16,256]{4,3,2,1,0:T(8,128)(2,1)S(1)}, bf16[4,3,2,16,256]{4,3,2,1,0:T(8,128)(2,1)}, u32[]{:S(2)}, u32[]{:S(2)}) collective-permute-start(bf16[4,3,2,16,256]{4,3,2,1,0:T(8,128)(2,1)S(1)} %collective-permute-done.11.near_ref), channel_id=1, source_target_pairs={{0,2},{2,4},{3,1},{4,6},{5,3},{7,5},{8,10},{10,12},{11,9},{12,14},... | collective-permute-start | bytes 589832 | tf_op jit(solution)/shard_map/ppermute | solution.py:386
  73.1 2.5 %collective-permute-done.12.far_ref = bf16[4,3,2,16,256]{4,3,2,1,0:T(8,128)(2,1)} collective-permute-done((bf16[4,3,2,16,256]{4,3,2,1,0:T(8,128)(2,1)S(1)}, bf16[4,3,2,16,256]{4,3,2,1,0:T(8,128)(2,1)}, u32[]{:S(2)}, u32[]{:S(2)}) %collective-permute-start.12) | collective-permute-done | bytes 196640 | tf_op jit(solution)/shard_map/ppermute | solution.py:386
  75.6 4.5 %collective-permute-start.7 = (bf16[8,3,2,16,256]{4,3,2,1,0:T(8,128)(2,1)}, bf16[8,3,2,16,256]{4,3,2,1,0:T(8,128)(2,1)S(1)}, u32[]{:S(2)}, u32[]{:S(2)}) collective-permute-start(bf16[8,3,2,16,256]{4,3,2,1,0:T(8,128)(2,1)} %collective-permute-done.6.near_ref), channel_id=1, source_target_pairs={{0,2},{2,4},{3,1},{4,6},{5,3},{7,5},{8,10},{10,12},{11,9},{12,14},... | collective-permute-start | bytes 1179656 | tf_op jit(solution)/shard_map/ppermute | solution.py:386
  80.1 0.0 collective-permute-done.9.near_ref
  80.1 4.2 %collective-permute-start.10 = (bf16[8,3,2,16,256]{4,3,2,1,0:T(8,128)(2,1)}, bf16[8,3,2,16,256]{4,3,2,1,0:T(8,128)(2,1)}, u32[]{:S(2)}, u32[]{:S(2)}) collective-permute-start(bf16[8,3,2,16,256]{4,3,2,1,0:T(8,128)(2,1)} %collective-permute-done.9.near_ref), channel_id=1, source_target_pairs={{0,2},{2,4},{3,1},{4,6},{5,3},{7,5},{8,10},{10,12},{11,9},{12,14},... | collective-permute-start | bytes 1179656 | tf_op jit(solution)/shard_map/ppermute | solution.py:386
  84.4 0.0 collective-permute-done.2.rest_1_
  84.4 3.6 %collective-permute-start.17 = (bf16[8,3,2,16,256]{4,3,2,1,0:T(8,128)(2,1)}, bf16[8,3,2,16,256]{4,3,2,1,0:T(8,128)(2,1)}, u32[]{:S(2)}, u32[]{:S(2)}) collective-permute-start(bf16[8,3,2,16,256]{4,3,2,1,0:T(8,128)(2,1)} %copy-done.9), channel_id=1, source_target_pairs={{0,2},{2,4},{3,1},{4,6},{5,3},{7,5},{8,10},{10,12},{11,9},{12,14},... | collective-permute-start | bytes 1179656 | tf_op jit(solution)/shard_map/ppermute | solution.py:386
  87.9 9.0 %local_terms.11 = (f32[2,2,16,256]{3,2,1,0:T(8,128)}, bf16[2,3,16,2,16,256]{5,4,3,2,1,0:T(8,128)(2,1)}) custom-call(s32[1]{0:T(128)} %bitcast.block_ref.me_ref, bf16[256,512]{1,0:T(8,128)(2,1)} %get-tuple-element.33.mix_ref, bf16[512,256]{1,0:T(8,128)(2,1)} %get-tuple-element.34.dcol_ref, bf16[2,128,256]{2,1,0:T(8,128)(2,1)} %get-tuple-element.35.drow_ref, ...), custom_call_target="tpu_custom_call" | custom-call | flops 2818572288 | bytes 11010048 | tf_op jit(solution)/shard_map/local_terms/pallas_call | solution.py:214
  96.9 1.6 %spread_rows.1 = (f32[2,2,4,1024]{3,2,1,0:T(4,128)}, f32[2,2,4,1024]{3,2,1,0:T(4,128)}, f32[2,2,4,1024]{3,2,1,0:T(4,128)}, f32[2,2,4,1024]{3,2,1,0:T(4,128)}) custom-call(s32[1]{0:T(128)} %bitcast.block_ref.me_ref, f32[2,2,16,256]{3,2,1,0:T(8,128)} %get-tuple-element.42.refs_0_, f32[2,2,16,256]{3,2,1,0:T(8,128)} %get-tuple-element.43.refs_1_, ...), custom_call_target="tpu_custom_call" | custom-call | tf_op jit(solution)/shard_map/spread_rows/pallas_call | solution.py:340
  98.5 0.0 collective-permute-done.7.far_ref
  98.6 1.3 %collective-permute-start.14 = (bf16[4,3,2,16,256]{4,3,2,1,0:T(8,128)(2,1)}, bf16[4,3,2,16,256]{4,3,2,1,0:T(8,128)(2,1)S(1)}, u32[]{:S(2)}, u32[]{:S(2)}) collective-permute-start(bf16[4,3,2,16,256]{4,3,2,1,0:T(8,128)(2,1)} %copy-done.11), channel_id=1, source_target_pairs={{0,2},{2,4},{3,1},{4,6},{5,3},{7,5},{8,10},{10,12},{11,9},{12,14},... | collective-permute-start | bytes 589832 | tf_op jit(solution)/shard_map/ppermute | solution.py:386
  99.9 0.0 collective-permute-done.10.far_ref
  99.9 0.1 collective-permute-start.5
  99.9 0.0 collective-permute-done.15.z1_ref
  100.0 1.6 %collective-permute-start.4 = (f32[2,2,4,1024]{3,2,1,0:T(4,128)}, f32[2,2,4,1024]{3,2,1,0:T(4,128)S(1)}, u32[]{:S(2)}, u32[]{:S(2)}) collective-permute-start(f32[2,2,4,1024]{3,2,1,0:T(4,128)} %get-tuple-element.50), channel_id=1, source_target_pairs={{0,16},{8,24},{16,0},{24,8},{1,17},{9,25},{17,1},{25,9},{2,18},{10... | collective-permute-start | bytes 196616 | tf_op jit(solution)/shard_map/ppermute | solution.py:383
  101.5 0.9 collective-permute-done.8.z1_ref
  102.5 0.0 collective-permute-start.3
  102.5 0.6 broadcast_select_fusion.coef_ref
  103.1 0.6 broadcast_in_dim.3.old_ref
  103.7 2.1 %depth_terms.9.old_ref = f32[2,16,256]{2,1,0:T(8,128)} custom-call(f32[8]{0:T(128)} %broadcast_select_fusion.coef_ref, bf16[8,3,2,16,256]{4,3,2,1,0:T(8,128)(2,1)} %get-tuple-element.52.own_ref, bf16[8,3,2,16,256]{4,3,2,1,0:T(8,128)(2,1)} %collective-permute-done.6.near_ref, bf16[8,3,2,16,256]{4,3,2,1,0:T(8,128)(2,1)} %copy-done.4, ...), custom_call_target="tpu_custom_call" | custom-call | tf_op jit(solution)/shard_map/depth_terms/pallas_call | solution.py:284
  105.8 2.1 %depth_terms.6.old_ref = f32[2,16,256]{2,1,0:T(8,128)} custom-call(f32[8]{0:T(128)} %broadcast_select_fusion.coef_ref, bf16[4,3,2,16,256]{4,3,2,1,0:T(8,128)(2,1)} %get-tuple-element.36.rest_0_.own_ref, bf16[4,3,2,16,256]{4,3,2,1,0:T(8,128)(2,1)} %copy-done.12, bf16[4,3,2,16,256]{4,3,2,1,0:T(8,128)(2,1)} %collective-permute-done.12.far_ref, ...), custom_call_target="tpu_custom_call" | custom-call | tf_op jit(solution)/shard_map/depth_terms/pallas_call | solution.py:284
  107.9 2.5 %depth_terms.7.old_ref = f32[2,16,256]{2,1,0:T(8,128)} custom-call(f32[8]{0:T(128)} %broadcast_select_fusion.coef_ref, bf16[8,3,2,16,256]{4,3,2,1,0:T(8,128)(2,1)} %get-tuple-element.54.own_ref, bf16[8,3,2,16,256]{4,3,2,1,0:T(8,128)(2,1)} %collective-permute-done.9.near_ref, bf16[8,3,2,16,256]{4,3,2,1,0:T(8,128)(2,1)} %collective-permute-done.10.far_ref, ...), custom_call_target="tpu_custom_call" | custom-call | tf_op jit(solution)/shard_map/depth_terms/pallas_call | solution.py:284
  110.4 2.1 %depth_terms.8.refs_0_ = f32[2,16,256]{2,1,0:T(8,128)} custom-call(f32[8]{0:T(128)} %broadcast_select_fusion.coef_ref, bf16[8,3,2,16,256]{4,3,2,1,0:T(8,128)(2,1)} %get-tuple-element.52.own_ref, bf16[8,3,2,16,256]{4,3,2,1,0:T(8,128)(2,1)} %collective-permute-done.6.near_ref, bf16[8,3,2,16,256]{4,3,2,1,0:T(8,128)(2,1)} %copy-done.4, ...), custom_call_target="tpu_custom_call" | custom-call | tf_op jit(solution)/shard_map/depth_terms/pallas_call | solution.py:284
  112.5 0.0 collective-permute-done.17.far_ref
  112.5 2.5 %depth_terms.10.old_ref = f32[2,16,256]{2,1,0:T(8,128)} custom-call(f32[8]{0:T(128)} %broadcast_select_fusion.coef_ref, bf16[8,3,2,16,256]{4,3,2,1,0:T(8,128)(2,1)} %get-tuple-element.56.own_ref, bf16[8,3,2,16,256]{4,3,2,1,0:T(8,128)(2,1)} %copy-done.9, bf16[8,3,2,16,256]{4,3,2,1,0:T(8,128)(2,1)} %collective-permute-done.17.far_ref, ...), custom_call_target="tpu_custom_call" | custom-call | tf_op jit(solution)/shard_map/depth_terms/pallas_call | solution.py:284
  115.0 0.0 collective-permute-done.14.far_ref
  115.0 0.7 copy-done.13
  115.7 2.1 %depth_terms.11.refs_1_ = f32[2,16,256]{2,1,0:T(8,128)} custom-call(f32[8]{0:T(128)} %broadcast_select_fusion.coef_ref, bf16[4,3,2,16,256]{4,3,2,1,0:T(8,128)(2,1)} %get-tuple-element.55.own_ref, bf16[4,3,2,16,256]{4,3,2,1,0:T(8,128)(2,1)} %copy-done.11, bf16[4,3,2,16,256]{4,3,2,1,0:T(8,128)(2,1)} %copy-done.13, ...), custom_call_target="tpu_custom_call" | custom-call | tf_op jit(solution)/shard_map/depth_terms/pallas_call | solution.py:284
  117.8 1.4 %cut_rows.1 = (f32[2,2,4,256]{3,2,1,0:T(4,128)}, f32[2,2,4,256]{3,2,1,0:T(4,128)}, f32[2,2,4,256]{3,2,1,0:T(4,128)}, f32[2,2,4,256]{3,2,1,0:T(4,128)}) custom-call(s32[1]{0:T(128)} %bitcast.block_ref.me_ref, f32[2,16,256]{2,1,0:T(8,128)} %depth_terms.8.refs_0_, f32[2,16,256]{2,1,0:T(8,128)} %depth_terms.11.refs_1_), custom_call_target="tpu_custom_call" | custom-call | tf_op jit(solution)/shard_map/cut_rows/pallas_call | solution.py:307
  119.2 0.5 collective-permute-start.18
  119.7 1.5 %collective-permute-start.19 = (f32[2,2,4,256]{3,2,1,0:T(4,128)}, f32[2,2,4,256]{3,2,1,0:T(4,128)S(1)}, u32[]{:S(2)}, u32[]{:S(2)}) collective-permute-start(f32[2,2,4,256]{3,2,1,0:T(4,128)} %get-tuple-element.59), channel_id=1, source_target_pairs={{0,16},{8,24},{16,0},{24,8},{1,17},{9,25},{17,1},{25,9},{2,18},{10... | collective-permute-start | bytes 49160 | tf_op jit(solution)/shard_map/ppermute | solution.py:383
  121.2 0.0 collective-permute-done.5
  121.2 0.0 collective-permute-start.20
  121.2 0.0 collective-permute-done.4
  121.2 0.0 collective-permute-done.3
  121.2 0.6 add_add_fusion
  121.9 1.8 %collective-permute-done.19.refs_2_ = f32[2,2,4,256]{3,2,1,0:T(4,128)S(1)} collective-permute-done((f32[2,2,4,256]{3,2,1,0:T(4,128)}, f32[2,2,4,256]{3,2,1,0:T(4,128)S(1)}, u32[]{:S(2)}, u32[]{:S(2)}) %collective-permute-start.19) | collective-permute-done | bytes 16416 | tf_op jit(solution)/shard_map/ppermute | solution.py:383
  123.6 1.1 collective-permute-done.20.refs_3_
  124.7 0.6 copy-done.17
  125.3 1.5 %join_columns.1 = f32[2,2,4,1024]{3,2,1,0:T(4,128)} custom-call(s32[1]{0:T(128)} %bitcast.block_ref.me_ref, f32[2,2,4,1024]{3,2,1,0:T(4,128)} %bitcast.11, f32[2,2,4,256]{3,2,1,0:T(4,128)} %get-tuple-element.57.refs_0_, f32[2,2,4,256]{3,2,1,0:T(4,128)} %copy-done.15, f32[2,2,4,256]{3,2,1,0:T(4,128)} %copy-done.16, f32[2,2,4,256]{3,2,1,0:T(4,128)} %copy-done.17), custom_call_target="tpu_custom_call" | custom-call | tf_op jit(solution)/shard_map/join_columns/pallas_call | solution.py:359
  (37 shorter events, 0.1 us)
Async XLA Ops:
  9.3 5.8 %collective-permute-start = (bf16[1,3,16,2,16,256]{5,4,3,2,1,0:T(8,128)(2,1)}, bf16[1,3,16,2,16,256]{5,4,3,2,1,0:T(8,128)(2,1)S(1)}, u32[]{:S(2)}, u32[]{:S(2)}) collective-permute-start(bf16[1,3,16,2,16,256]{5,4,3,2,1,0:T(8,128)(2,1)} %get-tuple-element.37.rest_0_), channel_id=1, source_target_pairs={{0,8},{8,0},{16,24},{24,16},{1,9},{9,1},{17,25},{25,17},{2,10},{10... | collective-permute-start | bytes 2359304 | tf_op jit(solution)/shard_map/ppermute | solution.py:383
  15.1 6.5 %collective-permute-start.1 = (bf16[1,3,16,2,16,256]{5,4,3,2,1,0:T(8,128)(2,1)}, bf16[1,3,16,2,16,256]{5,4,3,2,1,0:T(8,128)(2,1)S(1)}, u32[]{:S(2)}, u32[]{:S(2)}) collective-permute-start(bf16[1,3,16,2,16,256]{5,4,3,2,1,0:T(8,128)(2,1)} %get-tuple-element.38.rest_0_), channel_id=1, source_target_pairs={{0,8},{8,0},{16,24},{24,16},{1,9},{9,1},{17,25},{25,17},{2,10},{10... | collective-permute-start | bytes 2359304 | tf_op jit(solution)/shard_map/ppermute | solution.py:383
  15.2 0.9 copy-start.6
  21.5 0.9 copy-start.7
  27.9 9.1 %copy-start.3 = (bf16[8,3,2,16,256]{4,3,2,1,0:T(8,128)(2,1)S(1)}, bf16[8,3,2,16,256]{4,3,2,1,0:T(8,128)(2,1)}, u32[]{:S(2)}) copy-start(bf16[8,3,2,16,256]{4,3,2,1,0:T(8,128)(2,1)} %get-tuple-element.52.own_ref) | copy-start | bytes 1179652
  27.9 11.6 %copy-start.8 = (bf16[8,3,2,16,256]{4,3,2,1,0:T(8,128)(2,1)S(1)}, bf16[8,3,2,16,256]{4,3,2,1,0:T(8,128)(2,1)}, u32[]{:S(2)}) copy-start(bf16[8,3,2,16,256]{4,3,2,1,0:T(8,128)(2,1)} %get-tuple-element.56.own_ref) | copy-start | bytes 1179652
  27.9 11.7 %copy-start.10 = (bf16[4,3,2,16,256]{4,3,2,1,0:T(8,128)(2,1)S(1)}, bf16[4,3,2,16,256]{4,3,2,1,0:T(8,128)(2,1)}, u32[]{:S(2)}) copy-start(bf16[4,3,2,16,256]{4,3,2,1,0:T(8,128)(2,1)} %get-tuple-element.55.own_ref) | copy-start | bytes 589828
  27.9 13.7 %copy-start.5 = (bf16[4,3,2,16,256]{4,3,2,1,0:T(8,128)(2,1)S(1)}, bf16[4,3,2,16,256]{4,3,2,1,0:T(8,128)(2,1)}, u32[]{:S(2)}) copy-start(bf16[4,3,2,16,256]{4,3,2,1,0:T(8,128)(2,1)} %get-tuple-element.36.rest_0_.own_ref) | copy-start | bytes 589828
  36.6 47.8 %collective-permute-start.2 = (bf16[2,3,16,2,16,256]{5,4,3,2,1,0:T(8,128)(2,1)}, bf16[2,3,16,2,16,256]{5,4,3,2,1,0:T(8,128)(2,1)S(1)}, u32[]{:S(2)}, u32[]{:S(2)}) collective-permute-start(bf16[2,3,16,2,16,256]{5,4,3,2,1,0:T(8,128)(2,1)} %get-tuple-element.41.rest_0_), channel_id=1, source_target_pairs={{0,8},{8,0},{16,24},{24,16},{1,9},{9,1},{17,25},{25,17},{2,10},{10... | collective-permute-start | bytes 4718600 | tf_op jit(solution)/shard_map/ppermute | solution.py:383
  37.0 31.4 %collective-permute-start.6 = (bf16[8,3,2,16,256]{4,3,2,1,0:T(8,128)(2,1)S(1)}, bf16[8,3,2,16,256]{4,3,2,1,0:T(8,128)(2,1)}, u32[]{:S(2)}, u32[]{:S(2)}) collective-permute-start(bf16[8,3,2,16,256]{4,3,2,1,0:T(8,128)(2,1)S(1)} %copy-done.3), channel_id=1, source_target_pairs={{0,1},{1,0},{2,3},{3,2},{4,5},{5,4},{6,7},{7,6},{8,9},{9,8},{10,11... | collective-permute-start | bytes 1179656 | tf_op jit(solution)/shard_map/ppermute | solution.py:386
  39.6 28.9 %collective-permute-start.16 = (bf16[8,3,2,16,256]{4,3,2,1,0:T(8,128)(2,1)S(1)}, bf16[8,3,2,16,256]{4,3,2,1,0:T(8,128)(2,1)S(1)}, u32[]{:S(2)}, u32[]{:S(2)}) collective-permute-start(bf16[8,3,2,16,256]{4,3,2,1,0:T(8,128)(2,1)S(1)} %copy-done.8), channel_id=1, source_target_pairs={{0,1},{1,0},{2,3},{3,2},{4,5},{5,4},{6,7},{7,6},{8,9},{9,8},{10,11... | collective-permute-start | bytes 1179656 | tf_op jit(solution)/shard_map/ppermute | solution.py:386
  39.7 22.5 %collective-permute-start.13 = (bf16[4,3,2,16,256]{4,3,2,1,0:T(8,128)(2,1)S(1)}, bf16[4,3,2,16,256]{4,3,2,1,0:T(8,128)(2,1)S(1)}, u32[]{:S(2)}, u32[]{:S(2)}) collective-permute-start(bf16[4,3,2,16,256]{4,3,2,1,0:T(8,128)(2,1)S(1)} %copy-done.10), channel_id=1, source_target_pairs={{0,1},{1,0},{2,3},{3,2},{4,5},{5,4},{6,7},{7,6},{8,9},{9,8},{10,11... | collective-permute-start | bytes 589832 | tf_op jit(solution)/shard_map/ppermute | solution.py:386
  41.6 24.8 %collective-permute-start.11 = (bf16[4,3,2,16,256]{4,3,2,1,0:T(8,128)(2,1)S(1)}, bf16[4,3,2,16,256]{4,3,2,1,0:T(8,128)(2,1)S(1)}, u32[]{:S(2)}, u32[]{:S(2)}) collective-permute-start(bf16[4,3,2,16,256]{4,3,2,1,0:T(8,128)(2,1)S(1)} %copy-done.5), channel_id=1, source_target_pairs={{0,1},{1,0},{2,3},{3,2},{4,5},{5,4},{6,7},{7,6},{8,9},{9,8},{10,11... | collective-permute-start | bytes 589832 | tf_op jit(solution)/shard_map/ppermute | solution.py:386
  62.2 13.4 %copy-start.11 = (bf16[4,3,2,16,256]{4,3,2,1,0:T(8,128)(2,1)}, bf16[4,3,2,16,256]{4,3,2,1,0:T(8,128)(2,1)S(1)}, u32[]{:S(2)}) copy-start(bf16[4,3,2,16,256]{4,3,2,1,0:T(8,128)(2,1)S(1)} %collective-permute-done.13.near_ref) | copy-start | bytes 589828
  62.2 17.9 %collective-permute-start.9 = (bf16[8,3,2,16,256]{4,3,2,1,0:T(8,128)(2,1)}, bf16[8,3,2,16,256]{4,3,2,1,0:T(8,128)(2,1)}, u32[]{:S(2)}, u32[]{:S(2)}) collective-permute-start(bf16[8,3,2,16,256]{4,3,2,1,0:T(8,128)(2,1)} %get-tuple-element.54.own_ref), channel_id=1, source_target_pairs={{0,1},{1,0},{2,3},{3,2},{4,5},{5,4},{6,7},{7,6},{8,9},{9,8},{10,11... | collective-permute-start | bytes 1179656 | tf_op jit(solution)/shard_map/ppermute | solution.py:386
  66.4 13.7 %copy-start.12 = (bf16[4,3,2,16,256]{4,3,2,1,0:T(8,128)(2,1)}, bf16[4,3,2,16,256]{4,3,2,1,0:T(8,128)(2,1)S(1)}, u32[]{:S(2)}) copy-start(bf16[4,3,2,16,256]{4,3,2,1,0:T(8,128)(2,1)S(1)} %collective-permute-done.11.near_ref) | copy-start | bytes 589828
  66.4 33.6 %collective-permute-start.15 = (bf16[1,3,16,2,16,256]{5,4,3,2,1,0:T(8,128)(2,1)}, bf16[1,3,16,2,16,256]{5,4,3,2,1,0:T(8,128)(2,1)S(1)}, u32[]{:S(2)}, u32[]{:S(2)}) collective-permute-start(bf16[1,3,16,2,16,256]{5,4,3,2,1,0:T(8,128)(2,1)} %get-tuple-element.40.rest_0_), channel_id=1, source_target_pairs={{0,16},{8,24},{16,0},{24,8},{1,17},{9,25},{17,1},{25,9},{2,18},{10... | collective-permute-start | bytes 2359304 | tf_op jit(solution)/shard_map/ppermute | solution.py:383
  68.4 34.0 %collective-permute-start.8 = (bf16[1,3,16,2,16,256]{5,4,3,2,1,0:T(8,128)(2,1)}, bf16[1,3,16,2,16,256]{5,4,3,2,1,0:T(8,128)(2,1)S(1)}, u32[]{:S(2)}, u32[]{:S(2)}) collective-permute-start(bf16[1,3,16,2,16,256]{5,4,3,2,1,0:T(8,128)(2,1)} %get-tuple-element.39.rest_0_), channel_id=1, source_target_pairs={{0,16},{8,24},{16,0},{24,8},{1,17},{9,25},{17,1},{25,9},{2,18},{10... | collective-permute-start | bytes 2359304 | tf_op jit(solution)/shard_map/ppermute | solution.py:383
  68.5 4.6 %copy-start.9 = (bf16[8,3,2,16,256]{4,3,2,1,0:T(8,128)(2,1)}, bf16[8,3,2,16,256]{4,3,2,1,0:T(8,128)(2,1)S(1)}, u32[]{:S(2)}) copy-start(bf16[8,3,2,16,256]{4,3,2,1,0:T(8,128)(2,1)S(1)} %collective-permute-done.16.near_ref) | copy-start | bytes 1179652
  68.5 7.1 %collective-permute-start.12 = (bf16[4,3,2,16,256]{4,3,2,1,0:T(8,128)(2,1)S(1)}, bf16[4,3,2,16,256]{4,3,2,1,0:T(8,128)(2,1)}, u32[]{:S(2)}, u32[]{:S(2)}) collective-permute-start(bf16[4,3,2,16,256]{4,3,2,1,0:T(8,128)(2,1)S(1)} %collective-permute-done.11.near_ref), channel_id=1, source_target_pairs={{0,2},{2,4},{3,1},{4,6},{5,3},{7,5},{8,10},{10,12},{11,9},{12,14},... | collective-permute-start | bytes 589832 | tf_op jit(solution)/shard_map/ppermute | solution.py:386
  75.6 23.0 %collective-permute-start.7 = (bf16[8,3,2,16,256]{4,3,2,1,0:T(8,128)(2,1)}, bf16[8,3,2,16,256]{4,3,2,1,0:T(8,128)(2,1)S(1)}, u32[]{:S(2)}, u32[]{:S(2)}) collective-permute-start(bf16[8,3,2,16,256]{4,3,2,1,0:T(8,128)(2,1)} %collective-permute-done.6.near_ref), channel_id=1, source_target_pairs={{0,2},{2,4},{3,1},{4,6},{5,3},{7,5},{8,10},{10,12},{11,9},{12,14},... | collective-permute-start | bytes 1179656 | tf_op jit(solution)/shard_map/ppermute | solution.py:386
  80.1 19.7 %collective-permute-start.10 = (bf16[8,3,2,16,256]{4,3,2,1,0:T(8,128)(2,1)}, bf16[8,3,2,16,256]{4,3,2,1,0:T(8,128)(2,1)}, u32[]{:S(2)}, u32[]{:S(2)}) collective-permute-start(bf16[8,3,2,16,256]{4,3,2,1,0:T(8,128)(2,1)} %collective-permute-done.9.near_ref), channel_id=1, source_target_pairs={{0,2},{2,4},{3,1},{4,6},{5,3},{7,5},{8,10},{10,12},{11,9},{12,14},... | collective-permute-start | bytes 1179656 | tf_op jit(solution)/shard_map/ppermute | solution.py:386
  84.4 18.1 %copy-start.18 = (f32[8]{0:T(128)S(1)}, f32[8]{0:T(128)}, u32[]{:S(2)}) copy-start(f32[8]{0:T(128)} %constant.31.clone) | copy-start | bytes 100
  84.4 18.1 %copy-start.19 = (f32[8]{0:T(128)S(1)}, f32[8]{0:T(128)}, u32[]{:S(2)}) copy-start(f32[8]{0:T(128)} %constant.32.clone) | copy-start | bytes 100
  84.4 3.6 %copy-start.2 = (bf16[2,3,16,2,16,256]{5,4,3,2,1,0:T(8,128)(2,1)}, bf16[2,3,16,2,16,256]{5,4,3,2,1,0:T(8,128)(2,1)S(1)}, u32[]{:S(2)}) copy-start(bf16[2,3,16,2,16,256]{5,4,3,2,1,0:T(8,128)(2,1)S(1)} %collective-permute-done.2.rest_1_) | copy-start | bytes 4718596
  84.4 28.2 %collective-permute-start.17 = (bf16[8,3,2,16,256]{4,3,2,1,0:T(8,128)(2,1)}, bf16[8,3,2,16,256]{4,3,2,1,0:T(8,128)(2,1)}, u32[]{:S(2)}, u32[]{:S(2)}) collective-permute-start(bf16[8,3,2,16,256]{4,3,2,1,0:T(8,128)(2,1)} %copy-done.9), channel_id=1, source_target_pairs={{0,2},{2,4},{3,1},{4,6},{5,3},{7,5},{8,10},{10,12},{11,9},{12,14},... | collective-permute-start | bytes 1179656 | tf_op jit(solution)/shard_map/ppermute | solution.py:386
  98.5 5.1 %copy-start.4 = (bf16[8,3,2,16,256]{4,3,2,1,0:T(8,128)(2,1)}, bf16[8,3,2,16,256]{4,3,2,1,0:T(8,128)(2,1)S(1)}, u32[]{:S(2)}) copy-start(bf16[8,3,2,16,256]{4,3,2,1,0:T(8,128)(2,1)S(1)} %collective-permute-done.7.far_ref) | copy-start | bytes 1179652
  98.6 16.5 %collective-permute-start.14 = (bf16[4,3,2,16,256]{4,3,2,1,0:T(8,128)(2,1)}, bf16[4,3,2,16,256]{4,3,2,1,0:T(8,128)(2,1)S(1)}, u32[]{:S(2)}, u32[]{:S(2)}) collective-permute-start(bf16[4,3,2,16,256]{4,3,2,1,0:T(8,128)(2,1)} %copy-done.11), channel_id=1, source_target_pairs={{0,2},{2,4},{3,1},{4,6},{5,3},{7,5},{8,10},{10,12},{11,9},{12,14},... | collective-permute-start | bytes 589832 | tf_op jit(solution)/shard_map/ppermute | solution.py:386
  99.9 21.3 %collective-permute-start.5 = (f32[2,2,4,1024]{3,2,1,0:T(4,128)}, f32[2,2,4,1024]{3,2,1,0:T(4,128)S(1)}, u32[]{:S(2)}, u32[]{:S(2)}) collective-permute-start(f32[2,2,4,1024]{3,2,1,0:T(4,128)} %get-tuple-element.51), channel_id=1, source_target_pairs={{0,24},{8,16},{16,8},{24,0},{1,25},{9,17},{17,9},{25,1},{2,26},{10... | collective-permute-start | bytes 196616 | tf_op jit(solution)/shard_map/ppermute | solution.py:383
  100.0 3.7 %copy-start = (bf16[1,3,16,2,16,256]{5,4,3,2,1,0:T(8,128)(2,1)}, bf16[1,3,16,2,16,256]{5,4,3,2,1,0:T(8,128)(2,1)S(1)}, u32[]{:S(2)}) copy-start(bf16[1,3,16,2,16,256]{5,4,3,2,1,0:T(8,128)(2,1)S(1)} %collective-permute-done.15.z1_ref) | copy-start | bytes 2359300
  100.0 21.2 %collective-permute-start.4 = (f32[2,2,4,1024]{3,2,1,0:T(4,128)}, f32[2,2,4,1024]{3,2,1,0:T(4,128)S(1)}, u32[]{:S(2)}, u32[]{:S(2)}) collective-permute-start(f32[2,2,4,1024]{3,2,1,0:T(4,128)} %get-tuple-element.50), channel_id=1, source_target_pairs={{0,16},{8,24},{16,0},{24,8},{1,17},{9,25},{17,1},{25,9},{2,18},{10... | collective-permute-start | bytes 196616 | tf_op jit(solution)/shard_map/ppermute | solution.py:383
  102.5 3.3 %copy-start.1 = (bf16[1,3,16,2,16,256]{5,4,3,2,1,0:T(8,128)(2,1)}, bf16[1,3,16,2,16,256]{5,4,3,2,1,0:T(8,128)(2,1)S(1)}, u32[]{:S(2)}) copy-start(bf16[1,3,16,2,16,256]{5,4,3,2,1,0:T(8,128)(2,1)S(1)} %collective-permute-done.8.z1_ref) | copy-start | bytes 2359300
  102.5 18.7 %collective-permute-start.3 = (f32[2,2,4,1024]{3,2,1,0:T(4,128)}, f32[2,2,4,1024]{3,2,1,0:T(4,128)S(1)}, u32[]{:S(2)}, u32[]{:S(2)}) collective-permute-start(f32[2,2,4,1024]{3,2,1,0:T(4,128)} %get-tuple-element.49), channel_id=1, source_target_pairs={{0,8},{8,0},{16,24},{24,16},{1,9},{9,1},{17,25},{25,17},{2,10},{10... | collective-permute-start | bytes 196616 | tf_op jit(solution)/shard_map/ppermute | solution.py:383
  115.0 6.2 %copy-start.14 = (f32[2,2,4,1024]{3,2,1,0:T(4,128)S(1)}, f32[2,2,4,1024]{3,2,1,0:T(4,128)}, u32[]{:S(2)}) copy-start(f32[2,2,4,1024]{3,2,1,0:T(4,128)} %get-tuple-element.48) | copy-start | bytes 196612
  115.0 0.7 copy-start.13
  119.2 2.6 %collective-permute-start.18 = (f32[2,2,4,256]{3,2,1,0:T(4,128)}, f32[2,2,4,256]{3,2,1,0:T(4,128)S(1)}, u32[]{:S(2)}, u32[]{:S(2)}) collective-permute-start(f32[2,2,4,256]{3,2,1,0:T(4,128)} %get-tuple-element.58), channel_id=1, source_target_pairs={{0,8},{8,0},{16,24},{24,16},{1,9},{9,1},{17,25},{25,17},{2,10},{10... | collective-permute-start | bytes 49160 | tf_op jit(solution)/shard_map/ppermute | solution.py:383
  119.7 3.9 %collective-permute-start.19 = (f32[2,2,4,256]{3,2,1,0:T(4,128)}, f32[2,2,4,256]{3,2,1,0:T(4,128)S(1)}, u32[]{:S(2)}, u32[]{:S(2)}) collective-permute-start(f32[2,2,4,256]{3,2,1,0:T(4,128)} %get-tuple-element.59), channel_id=1, source_target_pairs={{0,16},{8,24},{16,0},{24,8},{1,17},{9,25},{17,1},{25,9},{2,18},{10... | collective-permute-start | bytes 49160 | tf_op jit(solution)/shard_map/ppermute | solution.py:383
  121.2 3.5 %collective-permute-start.20 = (f32[2,2,4,256]{3,2,1,0:T(4,128)}, f32[2,2,4,256]{3,2,1,0:T(4,128)S(1)}, u32[]{:S(2)}, u32[]{:S(2)}) collective-permute-start(f32[2,2,4,256]{3,2,1,0:T(4,128)} %get-tuple-element.60), channel_id=1, source_target_pairs={{0,24},{8,16},{16,8},{24,0},{1,25},{9,17},{17,9},{25,1},{2,26},{10... | collective-permute-start | bytes 49160 | tf_op jit(solution)/shard_map/ppermute | solution.py:383
  121.9 2.8 %copy-start.15 = (f32[2,2,4,256]{3,2,1,0:T(4,128)}, f32[2,2,4,256]{3,2,1,0:T(4,128)S(1)}, u32[]{:S(2)}) copy-start(f32[2,2,4,256]{3,2,1,0:T(4,128)S(1)} %collective-permute-done.18.refs_1_) | copy-start | bytes 49156
  123.6 1.1 copy-start.16
  124.7 0.6 copy-start.17

commit v2 on v0

v2 whole, which is shorter than its diff:
```python
import functools
import jax
import jax.numpy as jnp
import numpy as np
from jax import lax
from jax.experimental import pallas as pl
from jax.experimental.pallas import tpu as pltpu
from jax.sharding import PartitionSpec as P

LANES = 128
F32 = jnp.float32
BF16 = jnp.bfloat16
ANY = pl.BlockSpec(memory_space=pl.ANY)
SMEM = pl.BlockSpec(memory_space=pltpu.SMEM)
VMEM = pl.BlockSpec(memory_space=pltpu.VMEM)


def stencil(offset):
    return 8.0 * (offset == 1) - 8.0 * (offset == -1) - 1.0 * (offset == 2) + 1.0 * (offset == -2)


def stencils(snaps, rows, width):
    place = np.arange(width)
    dcol = stencil(place[:, None] - place[None, :])
    snap = np.arange(snaps)
    same = snap[:, None] == snap[None, :]
    drow = []
    for h in range(2):
        row = np.arange(rows // 2) + h * (rows // 2)
        band = stencil(np.arange(rows)[None, :] - row[:, None])
        drow.append(np.kron(same, band))
    return jnp.asarray(dcol, BF16), jnp.asarray(np.stack(drow), BF16)


def iota(shape, axis):
    return lax.broadcasted_iota(jnp.int32, shape, axis)


def in_vmem(x):
    return pltpu.with_memory_space_constraint(x, pltpu.VMEM)


def in_hbm(x):
    return pltpu.with_memory_space_constraint(x, pltpu.HBM)


def two_parts(high, low):
    return high.astype(F32) + low.astype(F32)


def over(x, n):
    if n & (n - 1):
        return lax.div(x, jnp.int32(n)), lax.rem(x, jnp.int32(n))
    return lax.shift_right_logical(x, jnp.int32(n.bit_length() - 1)), x & jnp.int32(n - 1)


def mm(a, b):
    return jnp.dot(a, b, preferred_element_type=F32)


def fill_mix(filters_ref, pairs_ref, mix_ref, rows):
    sources, stations, lags = filters_ref.shape
    points = mix_ref.shape[0] // sources
    snaps = points // rows
    depth = mix_ref.shape[1]
    shape = (snaps, stations * snaps)
    station, at = over(iota(shape, 1), snaps)
    lag = iota(shape, 0) - at + lags // 2
    spread = (over(iota((points, snaps), 0), rows)[0] == iota((points, snaps), 1)).astype(BF16)
    fan = (over(iota((depth // rows, depth), 1), rows)[0] == iota((depth // rows, depth), 0)).astype(BF16)
    same = over(iota((points, depth), 0), rows)[1] == over(iota((points, depth), 1), rows)[1]
    for e in range(sources):
        table = jnp.zeros(shape, F32)
        for r in range(stations):
            used = pairs_ref[e, r].astype(F32)
            for j in range(lags):
                table = jnp.where((station == r) & (lag == j), used * filters_ref[e, r, j], table)
        high = table.astype(BF16)
        low = (table - high.astype(F32)).astype(BF16)
        taps = jnp.concatenate([high, low], axis=1)
        full = mm(mm(spread, taps).astype(BF16), fan)
        mix_ref[pl.ds(e * points, points)] = jnp.where(same, full, 0.0).astype(BF16)


def prepare(displacement, lam, mu, me, slab, width, sizes, filters, pairs):
    sources, snaps, comps, planes, rows, _ = displacement.shape
    stations = filters.shape[1]
    points = snaps * rows // 2
    pieces = len(sizes)
    marks = [divmod(sum(sizes[:k]), snaps) for k in range(pieces)]
    fixed = stencils(snaps, rows, width)

    def kernel(me_ref, slab_ref, filters_ref, pairs_ref, src, *rest):
        ins, outs, (u_ref, *copies), mix_ref, sems = rest[:4], rest[4 : 4 + pieces], rest[4 + pieces : -2], rest[-2], rest[-1]
        here = pl.ds(pl.multiple_of(me_ref[0] * width, width), width)
        spans = [(e, pl.ds(s, size)) for (e, s), size in zip(marks, sizes)]
        gets = [pltpu.make_async_copy(src.at[span], u_ref.at[span], sems.at[0, k]) for k, span in enumerate(spans)]
        puts = [
            pltpu.make_async_copy(u_ref.at[span + (slice(None),) * 3 + (here,)], outs[k], sems.at[1, k])
            for k, span in enumerate(spans)
        ]
        others = [pltpu.make_async_copy(a, b, sems.at[2, k]) for k, (a, b) in enumerate(zip(ins, copies))]
        for copy in gets + others:
            copy.start()
        fill_mix(filters_ref, pairs_ref, mix_ref, rows // 2)
        for get, put in zip(gets, puts):
            get.wait()
            put.start()
        for copy in others + puts:
            copy.wait()

    hbm = (lam, mu) + fixed
    out = pl.pallas_call(
        kernel,
        out_shape=[jax.ShapeDtypeStruct((size, comps, planes, rows, width), displacement.dtype) for size in sizes]
        + [pltpu.VMEM(array.shape, array.dtype) for array in (displacement,) + hbm]
        + [pltpu.VMEM((sources * points, 4 * stations * points // 2), BF16)],
        in_specs=[SMEM] * 4 + [ANY] * 5,
        out_specs=[ANY] * pieces + [VMEM] * 6,
        scratch_shapes=[pltpu.SemaphoreType.DMA((3, max(pieces, 4)))],
        cost_estimate=pl.CostEstimate(
            flops=0, bytes_accessed=int(8 * displacement.size * displacement.dtype.itemsize), transcendentals=0
        ),
        compiler_params=pltpu.CompilerParams(vmem_limit_bytes=8 * 2**20),
        name="prepare",
    )(me, slab, in_hbm(filters), in_hbm(pairs), in_hbm(displacement), *map(in_hbm, hbm))
    pieces_out, (u, lam, mu, dcol, drow, mix) = out[:pieces], out[pieces:]
    return pieces_out, (mix, dcol, drow), u, lam, mu


def local_kernel(
    me_ref, mix_ref, dcol_ref, drow_ref, green_ref, u_ref, lam_ref, mu_ref, *rest, bits, first, waits, more
):
    added = rest[waits : waits + more]
    z_ref, gs, xs, ys = rest[waits + more :]
    count, _, planes, rows, width = z_ref.shape
    stations, snaps = green_ref.shape[:2]
    cols = u_ref.shape[-1]
    half = rows // 2
    points = snaps * half
    block = me_ref[0] ^ bits
    here = pl.ds(pl.multiple_of(block * width, width), width)
    before = pl.ds(pl.multiple_of(jnp.maximum(block * width - LANES, 0), LANES), LANES)
    behind = pl.ds(pl.multiple_of(jnp.minimum(block * width + width, cols - LANES), LANES), LANES)
    span = lambda h: pl.ds(h * half, half)
    space = lambda unit, size: pltpu.ACC(unit)((size, width), F32)

    lane = iota((half, LANES), 1)
    inner_left = jnp.where(block == 0, 0.0, 1.0)
    inner_right = jnp.where(block == cols // width - 1, 0.0, 1.0)
    left_2 = jnp.where(lane < 2, 1.0, 0.0) * inner_left
    left_1 = jnp.where(lane == 0, -8.0, 0.0) * inner_left
    right_2 = jnp.where(lane >= LANES - 2, -1.0, 0.0) * inner_right
    right_1 = jnp.where(lane == LANES - 1, 8.0, 0.0) * inner_right

    def one(index, carry):
        now, e = over(index, count)
        quake = first + e

        def filtered(h):
            def run(*accs):
                for k in range(3):
                    for unit in range(2):
                        tile = green_ref[:, :, 2 * k + unit, now, span(h), here].reshape(stations * points, width)
                        pltpu.matmul_push_rhs(tile, staging_register=k % 2, mxu_index=unit)
                    for part in range(2):
                        row = pl.ds(pl.multiple_of(quake * points, points), points)
                        lhs = mix_ref[row, pl.ds(part * stations * points, stations * points)]
                        for unit in range(2):
                            acc = accs[2 * unit + k % 2]
                            pltpu.matmul_acc_lhs(acc, lhs, load_staged_rhs=k % 2 if part == 0 else None)
                    for unit in range(2):
                        gs[2 * k + unit, h] = pltpu.matmul_pop(accs[2 * unit + k % 2])

            pl.run_scoped(run, *[space(unit, points) for unit in range(2) for _ in range(2)])

        whole = [u_ref[quake, :, i, now, :, here].reshape(2 * points, width) for i in range(3)]

        def columns(*accs):
            for unit in range(2):
                pltpu.matmul_push_rhs(dcol_ref[...], staging_register=0, mxu_index=unit)
            for unit in range(2):
                pltpu.matmul_acc_lhs(accs[2 * unit], whole[unit], load_staged_rhs=0)
                pltpu.matmul_acc_lhs(accs[2 * unit + 1], whole[2][unit * points : (unit + 1) * points])
            for unit in range(2):
                xs[unit] = pltpu.matmul_pop(accs[2 * unit])
                xs[2, pl.ds(unit * points, points)] = pltpu.matmul_pop(accs[2 * unit + 1])

        def lines(*accs):
            for unit in range(2):
                pltpu.matmul_push_rhs(whole[unit], staging_register=0, mxu_index=unit)
                pltpu.matmul_push_rhs(whole[2], staging_register=1, mxu_index=unit)
            for unit in range(2):
                pltpu.matmul_acc_lhs(accs[3 * unit], drow_ref[0], load_staged_rhs=0)
                pltpu.matmul_acc_lhs(accs[3 * unit + 1], drow_ref[1])
                pltpu.matmul_acc_lhs(accs[3 * unit + 2], drow_ref[unit], load_staged_rhs=1)
            for unit in range(2):
                ys[unit, 0] = pltpu.matmul_pop(accs[3 * unit])
                ys[unit, 1] = pltpu.matmul_pop(accs[3 * unit + 1])
                ys[2, unit] = pltpu.matmul_pop(accs[3 * unit + 2])

        def along_columns(i, s, h):
            left = u_ref[quake, s, i, now, span(h), before].astype(F32)
            right = u_ref[quake, s, i, now, span(h), behind].astype(F32)
            left = pltpu.roll(left, 2, 1) * left_2 + pltpu.roll(left, 1, 1) * left_1
            right = pltpu.roll(right, LANES - 2, 1) * right_2 + pltpu.roll(right, LANES - 1, 1) * right_1
            inside = xs[i, pl.ds((2 * s + h) * half, half)]
            middle = inside[:, LANES : width - LANES]
            parts = [inside[:, :LANES] + left] + ([middle] if middle.shape[1] else [])
            return jnp.concatenate(parts + [inside[:, width - LANES :] + right], axis=1)

        def combine(h):
            vol = dev = jnp.zeros((half, width), F32)
            lam = lam_ref[now, span(h), here]
            mu2 = 2.0 * mu_ref[now, span(h), here]
            for s in range(snaps):
                at = pl.ds(s * half, half)
                xs0, xs1, xs2 = (along_columns(i, s, h) for i in range(3))
                gxx, gyy, gzz, gyz, gxz, gxy = (gs[c, h, at] for c in range(6))
                gtr = gxx + gyy + gzz
                dxx, dyy = xs0, ys[1, h, at]
                vol = vol + (dxx + dyy) * gtr
                dev = dev + (dxx * gxx + dyy * gyy) + (ys[2, h, at] * gyz + xs2 * gxz)
                dev = dev + (xs1 + ys[0, h, at]) * gxy
                for i, z in enumerate((mu2 * gxz, mu2 * gyz, lam * gtr + mu2 * gzz)):
                    for ref in added:
                        z = z + ref[e, i * snaps + s, now, span(h)].astype(F32)
                    z_ref[e, i * snaps + s, now, span(h)] = z.astype(BF16)
            part = (lam * vol + mu2 * dev) / 12.0
            for ref in added:
                part = part + two_parts(ref[e, 3 * snaps, now, span(h)], ref[e, 3 * snaps + 1, now, span(h)])
            high = part.astype(BF16)
            z_ref[e, 3 * snaps, now, span(h)] = high
            z_ref[e, 3 * snaps + 1, now, span(h)] = (part - high.astype(F32)).astype(BF16)

        pl.run_scoped(columns, *[space(unit, size) for unit in range(2) for size in (2 * points, points)])
        pl.run_scoped(lines, *[space(unit, points) for unit in range(2) for _ in range(3)])
        filtered(0)
        filtered(1)
        combine(0)
        combine(1)
        return carry

    lax.fori_loop(0, planes * count, one, 0)


def local_terms(me, bits, first, count, mats, green, displacement, lam, mu, width, after=(), add=()):
    _, snaps, _, planes, rows, _ = displacement.shape
    stations = green.shape[0]
    points = snaps * rows
    return pl.pallas_call(
        functools.partial(local_kernel, bits=bits, first=first, waits=len(after), more=len(add)),
        out_shape=jax.ShapeDtypeStruct((count, 3 * snaps + 2, planes, rows, width), BF16),
        in_specs=[SMEM] + [VMEM] * 7 + [ANY] * len(after) + [VMEM] * len(add),
        out_specs=VMEM,
        scratch_shapes=[
            pltpu.VMEM((6, 2, points // 2, width), F32),
            pltpu.VMEM((3, points, width), F32),
            pltpu.VMEM((3, 2, points // 2, width), F32),
        ],
        cost_estimate=pl.CostEstimate(
            flops=int(count * planes * 2 * width * points * (6 * stations * points + 3 * width + 3 * points)),
            bytes_accessed=int(count * planes * width * rows * snaps * (6 * stations + 9) * 2),
            transcendentals=0,
        ),
        compiler_params=pltpu.CompilerParams(vmem_limit_bytes=16 * 2**20),
        name="local_terms",
    )(me, *mats, in_vmem(green), displacement, lam, mu, *after, *map(in_vmem, add))


def depth_kernel(me_ref, slab_ref, *refs, groups, slabs, lasts):
    pieces, rest = refs[:lasts[0]], refs[lasts[0] :]
    z0_ref, z1_ref, outs = rest[0], rest[1], rest[2:]
    _, rows, width = z1_ref.shape[2:]
    source = lasts[1]
    snaps = (z1_ref.shape[1] - 2) // 3
    slab = slab_ref[0]
    even = slab % 2 == 0
    known = jnp.where(even, slab > 0, slab < slabs - 1).astype(F32)
    pick = lambda one, other: jnp.where(even, jnp.float32(one), jnp.float32(other))
    coefs = [pick(*both) for both in ((-1, 1), (0, -8), (1, -1), (-8, 0), (8, 0), (-1, 1), (0, 8), (1, -1))]
    coefs = [coef * known if k % 4 >= 2 else coef for k, coef in enumerate(coefs)]
    total = [
        sum(two_parts(ref[k, 3 * snaps, p], ref[k, 3 * snaps + 1, p]) for ref, k in ((z0_ref, source), (z1_ref, 0)))
        for p in range(2)
    ]
    carry = tuple(jnp.zeros((rows, width), F32) for _ in range(2))
    at = 0
    for own_ref, near_ref, far_ref in zip(pieces[0::3], pieces[1::3], pieces[2::3]):

        def step(s, carry, at=at, own_ref=own_ref, near_ref=near_ref, far_ref=far_ref):
            top, bottom = carry
            for i in range(3):
                own0, own1 = own_ref[s, i, 0].astype(F32), own_ref[s, i, 1].astype(F32)
                n0, n1 = near_ref[s, i, 0].astype(F32), near_ref[s, i, 1].astype(F32)
                f0, f1 = far_ref[s, i, 0].astype(F32), far_ref[s, i, 1].astype(F32)
                d0 = 8.0 * own1 + (coefs[0] * n0 + coefs[1] * n1) + (coefs[2] * f0 + coefs[3] * f1)
                d1 = (coefs[4] * n0 + coefs[5] * n1) + (coefs[6] * f0 + coefs[7] * f1) - 8.0 * own0
                k = i * snaps + at + s
                z = [z0_ref[source, k, p].astype(F32) + z1_ref[0, k, p].astype(F32) for p in range(2)]
                top = top + z[0] * d0
                bottom = bottom + z[1] * d1
            return top, bottom

        count = own_ref.shape[0]
        carry = lax.fori_loop(0, count, step, carry, unroll=2)
        at += count
    part = rows // groups
    held = outs[-1]
    for p in range(2):
        value = total[p] + carry[p] / 12.0
        for q in range(groups):
            held[q, p] = value[q * part : (q + 1) * part]
    for bits, out in enumerate(outs[:-1]):
        out[...] = held[me_ref[0] ^ bits]


def depth_terms(me, slab, pieces, z0, z1, source, groups, slabs):
    planes, rows, width = z1.shape[2:]
    shape = (planes, rows // groups, width)
    flat = [array for piece in pieces for array in piece]
    return pl.pallas_call(
        functools.partial(depth_kernel, groups=groups, slabs=slabs, lasts=(len(flat), source)),
        out_shape=[jax.ShapeDtypeStruct(shape, F32)] * groups,
        in_specs=[SMEM, SMEM] + [VMEM] * (len(flat) + 2),
        out_specs=[VMEM] * groups,
        scratch_shapes=[pltpu.VMEM((groups,) + shape, F32)],
        compiler_params=pltpu.CompilerParams(vmem_limit_bytes=8 * 2**20),
        name="depth_terms",
    )(me, slab, *map(in_vmem, flat + [z0, z1]))


def join_kernel(me_ref, *refs):
    pieces, out = refs[:-1], refs[-1]
    sources = out.shape[0]
    width = pieces[0].shape[-1]
    for k, piece in enumerate(pieces):
        bits, e = divmod(k, sources)
        out[e, :, :, pl.ds(pl.multiple_of((me_ref[0] ^ bits) * width, width), width)] = piece[...]


def join_columns(me, pieces, sources):
    planes, part, width = pieces[0].shape
    return pl.pallas_call(
        join_kernel,
        out_shape=jax.ShapeDtypeStruct((sources, planes, part, width * len(pieces) // sources), F32),
        in_specs=[SMEM] + [VMEM] * len(pieces),
        out_specs=VMEM,
        compiler_params=pltpu.CompilerParams(vmem_limit_bytes=8 * 2**20),
        name="join_columns",
    )(me, *map(in_vmem, pieces))


SHARES = (1, 1, 1, 1)


def on_device(displacement, green, lame_lambda, shear_modulus, filters, pairs):
    sources, snaps, _, _, _, cols = displacement.shape
    groups = lax.axis_size("rcv")
    slabs = lax.axis_size("slab")
    me = lax.axis_index("rcv").reshape(1)
    slab = lax.axis_index("slab").reshape(1)
    width = cols // groups
    pair_swap = [(i, i ^ 1) for i in range(slabs)]
    onward = [(i, (i + 2 if i % 2 == 0 else i - 2) % slabs) for i in range(slabs)]

    def swap(x, bit):
        return lax.ppermute(x, "rcv", [(i, i ^ bit) for i in range(groups)])

    def along(x, links):
        return lax.ppermute(x, "slab", links)

    def terms(bits, first, count, after=(), add=()):
        return local_terms(
            me, bits, first, count, mats, green, u, lam, mu, width, after, add
        )

    total_snaps = sources * snaps
    unit = total_snaps // sum(SHARES)
    sizes = [share * unit for share in SHARES]
    own, mats, u, lam, mu = prepare(displacement, lame_lambda, shear_modulus, me, slab, width, sizes, filters, pairs)
    near = [along(piece, pair_swap) for piece in own]
    far = [along(piece, onward) for piece in near]

    across = []
    last = own[0]
    for e in range(sources):
        last = terms(3, e, 1, (last,))
        sent = swap(last, 1)
        last = terms(2, e, 1, (last,), (sent,))
        across.append(swap(last, 2))
    last = terms(1, 0, sources, (last,))
    z0 = terms(0, 0, sources, (last,), (swap(last, 1),))

    pieces = []
    for e in range(sources):
        mine = [k for k in range(len(SHARES)) if sum(sizes[:k]) // snaps == e]
        pieces.append(depth_terms(me, slab, [(own[k], near[k], far[k]) for k in mine], z0, across[e], e, groups, slabs))
    ends = []
    for bits in range(groups):
        for e in range(sources):
            piece = pieces[e][bits]
            ends.append(swap(piece, bits) if bits else piece)
    return join_columns(me, ends, sources)


def solution(mesh):
    placed = (
        P(None, None, None, "slab", None, None),
        P("rcv", None, None, "slab", None, None),
        P("slab", None, None),
        P("slab", None, None),
        P(None, "rcv", None),
        P(None, "rcv"),
    )
    return jax.shard_map(
        on_device,
        mesh=mesh,
        in_specs=placed,
        out_specs=P(None, "slab", "rcv", None),
        check_vma=False,
    )
```

time: 496 us -> 100 us (0.20)
  other arithmetic: 241 us -> 0 us
  waiting for transfers between devices: 181 us -> 50.6 us
  local copies, waits for them, and re-layouts: 49.5 us -> 4.57 us
  Pallas kernels: 0 us -> 24.2 us
  starting transfers between devices: 6.31 us -> 20.9 us
  between operations: 14.2 us -> 0.1 us
    reduce_sum x4 -> x0, other arithmetic: 125 us -> none  [contribution(): jnp.sum(filtered * green_one.astype(jnp.float32) * weights, axis=(0, 1))]
    all_gather x1 -> x0, waiting for transfers between devices: 84.3 us -> none  [on_device(): every_edge = lax.all_gather(edges, 'rcv', axis=0, tiled=True)]
    div x2 -> x0, other arithmetic: 75 us -> none  [the longest x1 43.1 us: derivative(): return (8.0 * (window(1) - window(-1)) - (window(2) - window(-2))) / 12.0]
    unnamed x3 -> x0, waiting for transfers between devices: 31.2 us -> none
    squeeze x4 -> x0, local copies, waits for them, and re-layouts: 27.1 us -> none  [add_slot(): stress_one = lax.dynamic_index_in_dim(stress, source, 0, keepdims=False)]
    pallas_call x0 -> x10, Pallas kernels: none -> 24.2 us  [the longest x6 17.9 us: local_terms(): pl.pallas_call(functools.partial(local_kernel, bits=bits, first=first, wa...]
    unnamed x6 -> x0, other arithmetic: 21.3 us -> none
    ppermute x2 -> x19, waiting for transfers between devices: 65.9 us -> 50.6 us  [the longest x8 44 us: along(): return lax.ppermute(x, 'slab', links)]
  transfers between devices with their start and end apart: 4 -> 19, of which waited for: 3 -> 12; matrix products, arithmetic and copies ran while one was open for 0% -> 0% of each run, Pallas kernels for 0% -> 6%
where the time goes in v2:
time: 100 us
  waiting for transfers between devices  50.6 us (51%)
  Pallas kernels  24.2 us (24%)
  starting transfers between devices  20.9 us (21%)
  local copies, waits for them, and re-layouts  4.57 us (5%)
    ppermute x8, waiting for transfers between devices, along(): return lax.ppermute(x, 'slab', links)  44 us
    pallas_call x6, Pallas kernels, local_terms(): pl.pallas_call(functools.partial(local_kernel, bits=bits, first=first, wa...  17.9 us
    ppermute x8, starting transfers between devices, along(): return lax.ppermute(x, 'slab', links)  11.9 us
    ppermute x11, starting transfers between devices, swap(): return lax.ppermute(x, 'rcv', [(i, i ^ bit) for i in range(groups)])  8.98 us
    ppermute x11, waiting for transfers between devices, swap(): return lax.ppermute(x, 'rcv', [(i, i ^ bit) for i in range(groups)])  6.55 us
    unnamed x4, local copies, waits for them, and re-layouts  4.57 us
    pallas_call x1, Pallas kernels, prepare(): pl.pallas_call(kernel, out_shape=[jax.ShapeDtypeStruct((size, comps, plan...  3.74 us
  transfers between devices with their start and end apart: 19, of which 12 were waited for; matrix products, arithmetic and copies ran while one was open for 0% of the time, Pallas kernels for 6%

profile of v2, /device:TPU:0, one launch (start us, length us, event | category | flops | bytes accessed | tf_op | source)
XLA Modules:
  0.0 100.2 jit_solution(1339636536129086321)
XLA Ops:
  0.0 3.7 %prepare.1 = (bf16[8,3,2,16,256]{4,3,2,1,0:T(8,128)(2,1)S(1)}, bf16[8,3,2,16,256]{4,3,2,1,0:T(8,128)(2,1)S(1)}, bf16[8,3,2,16,256]{4,3,2,1,0:T(8,128)(2,1)S(1)},...) custom-call(s32[1]{0:T(128)} %bitcast.me_ref, ...), custom_call_target="tpu_custom_call" | custom-call | bytes 50331648 | tf_op jit(solution)/shard_map/prepare/pallas_call | solution.py:113
  3.7 0.0 copy-start
  3.8 4.6 %copy-done = bf16[2,16,6,2,16,1024]{5,4,3,2,1,0:T(8,128)(2,1)S(1)} copy-done((bf16[2,16,6,2,16,1024]{5,4,3,2,1,0:T(8,128)(2,1)S(1)}, bf16[2,16,6,2,16,1024]{5,4,3,2,1,0:T(8,128)(2,1)}, u32[]{:S(2)}) %copy-start) | copy-done | bytes 12582936
  8.3 0.0 copy-start.1
  8.3 2.1 %local_terms.6.rest_0_ = bf16[1,50,2,16,256]{4,3,2,1,0:T(8,128)(2,1)S(1)} custom-call(s32[1]{0:T(128)} %bitcast.me_ref, bf16[256,512]{1,0:T(8,128)(2,1)S(1)} %get-tuple-element.25.mix_ref, bf16[256,256]{1,0:T(8,128)(2,1)S(1)} %get-tuple-element.26.dcol_ref, bf16[2,128,256]{2,1,0:T(8,128)(2,1)S(1)} %get-tuple-element.27.drow_ref, ...), custom_call_target="tpu_custom_call" | custom-call | flops 1207959552 | bytes 5505024 | tf_op jit(solution)/shard_map/local_terms/pallas_call | solution.py:251
  10.5 0.6 collective-permute-start.4
  11.1 2.0 %collective-permute-done.4.rest_1_ = bf16[1,50,2,16,256]{4,3,2,1,0:T(8,128)(2,1)S(1)} collective-permute-done((bf16[1,50,2,16,256]{4,3,2,1,0:T(8,128)(2,1)S(1)}, bf16[1,50,2,16,256]{4,3,2,1,0:T(8,128)(2,1)S(1)}, u32[]{:S(2)}, u32[]{:S(2)}) %collective-permute-start.4) | collective-permute-done | bytes 819232 | tf_op jit(solution)/shard_map/ppermute | solution.py:368
  13.0 0.0 copy-done.1
  13.0 2.3 %local_terms.7.rest_0_ = bf16[1,50,2,16,256]{4,3,2,1,0:T(8,128)(2,1)S(1)} custom-call(s32[1]{0:T(128)} %bitcast.me_ref, bf16[256,512]{1,0:T(8,128)(2,1)S(1)} %get-tuple-element.25.mix_ref, bf16[256,256]{1,0:T(8,128)(2,1)S(1)} %get-tuple-element.26.dcol_ref, bf16[2,128,256]{2,1,0:T(8,128)(2,1)S(1)} %get-tuple-element.27.drow_ref, ...), custom_call_target="tpu_custom_call" | custom-call | flops 1207959552 | bytes 5505024 | tf_op jit(solution)/shard_map/local_terms/pallas_call | solution.py:251
  15.3 2.2 %local_terms.8.rest_0_ = bf16[1,50,2,16,256]{4,3,2,1,0:T(8,128)(2,1)S(1)} custom-call(s32[1]{0:T(128)} %bitcast.me_ref, bf16[256,512]{1,0:T(8,128)(2,1)S(1)} %get-tuple-element.25.mix_ref, bf16[256,256]{1,0:T(8,128)(2,1)S(1)} %get-tuple-element.26.dcol_ref, bf16[2,128,256]{2,1,0:T(8,128)(2,1)S(1)} %get-tuple-element.27.drow_ref, ...), custom_call_target="tpu_custom_call" | custom-call | flops 1207959552 | bytes 5505024 | tf_op jit(solution)/shard_map/local_terms/pallas_call | solution.py:251
  17.5 0.4 collective-permute-start.5
  17.9 2.0 %collective-permute-done.5.rest_1_ = bf16[1,50,2,16,256]{4,3,2,1,0:T(8,128)(2,1)S(1)} collective-permute-done((bf16[1,50,2,16,256]{4,3,2,1,0:T(8,128)(2,1)S(1)}, bf16[1,50,2,16,256]{4,3,2,1,0:T(8,128)(2,1)S(1)}, u32[]{:S(2)}, u32[]{:S(2)}) %collective-permute-start.5) | collective-permute-done | bytes 819232 | tf_op jit(solution)/shard_map/ppermute | solution.py:368
  19.9 2.3 %local_terms.9.rest_0_ = bf16[1,50,2,16,256]{4,3,2,1,0:T(8,128)(2,1)S(1)} custom-call(s32[1]{0:T(128)} %bitcast.me_ref, bf16[256,512]{1,0:T(8,128)(2,1)S(1)} %get-tuple-element.25.mix_ref, bf16[256,256]{1,0:T(8,128)(2,1)S(1)} %get-tuple-element.26.dcol_ref, bf16[2,128,256]{2,1,0:T(8,128)(2,1)S(1)} %get-tuple-element.27.drow_ref, ...), custom_call_target="tpu_custom_call" | custom-call | flops 1207959552 | bytes 5505024 | tf_op jit(solution)/shard_map/local_terms/pallas_call | solution.py:251
  22.2 4.4 %local_terms.10.rest_0_ = bf16[2,50,2,16,256]{4,3,2,1,0:T(8,128)(2,1)S(1)} custom-call(s32[1]{0:T(128)} %bitcast.me_ref, bf16[256,512]{1,0:T(8,128)(2,1)S(1)} %get-tuple-element.25.mix_ref, bf16[256,256]{1,0:T(8,128)(2,1)S(1)} %get-tuple-element.26.dcol_ref, bf16[2,128,256]{2,1,0:T(8,128)(2,1)S(1)} %get-tuple-element.27.drow_ref, ...), custom_call_target="tpu_custom_call" | custom-call | flops 2415919104 | bytes 11010048 | tf_op jit(solution)/shard_map/local_terms/pallas_call | solution.py:251
  26.6 0.4 collective-permute-start.6
  27.0 2.6 %collective-permute-start.10 = (bf16[8,3,2,16,256]{4,3,2,1,0:T(8,128)(2,1)S(1)}, bf16[8,3,2,16,256]{4,3,2,1,0:T(8,128)(2,1)S(1)}, u32[]{:S(2)}, u32[]{:S(2)}) collective-permute-start(bf16[8,3,2,16,256]{4,3,2,1,0:T(8,128)(2,1)S(1)} %get-tuple-element.33.refs_3_), channel_id=1, source_target_pairs={{0,1},{1,0},{2,3},{3,2},{4,5},{5,4},{6,7},{7,6},{8,9},{9,8},{10,11... | collective-permute-start | bytes 1179656 | tf_op jit(solution)/shard_map/ppermute | solution.py:371
  29.6 0.1 collective-permute-start.8
  29.7 2.0 %collective-permute-start = (bf16[8,3,2,16,256]{4,3,2,1,0:T(8,128)(2,1)S(1)}, bf16[8,3,2,16,256]{4,3,2,1,0:T(8,128)(2,1)S(1)}, u32[]{:S(2)}, u32[]{:S(2)}) collective-permute-start(bf16[8,3,2,16,256]{4,3,2,1,0:T(8,128)(2,1)S(1)} %get-tuple-element.23.rest_0_.refs_0_), channel_id=1, source_target_pairs={{0,1},{1,0},{2,3},{3,2},{4,5},{5,4},{6,7},{7,6},{8,9},{9,8},{10,11... | collective-permute-start | bytes 1179656 | tf_op jit(solution)/shard_map/ppermute | solution.py:371
  31.6 1.6 %collective-permute-start.12 = (bf16[1,50,2,16,256]{4,3,2,1,0:T(8,128)(2,1)S(1)}, bf16[1,50,2,16,256]{4,3,2,1,0:T(8,128)(2,1)S(1)}, u32[]{:S(2)}, u32[]{:S(2)}) collective-permute-start(bf16[1,50,2,16,256]{4,3,2,1,0:T(8,128)(2,1)S(1)} %local_terms.9.rest_0_), channel_id=1, source_target_pairs={{0,16},{8,24},{16,0},{24,8},{1,17},{9,25},{17,1},{25,9},{2,18},{10... | collective-permute-start | bytes 2457608 | tf_op jit(solution)/shard_map/ppermute | solution.py:368
  33.3 6.3 %collective-permute-done.10.refs_4_ = bf16[8,3,2,16,256]{4,3,2,1,0:T(8,128)(2,1)S(1)} collective-permute-done((bf16[8,3,2,16,256]{4,3,2,1,0:T(8,128)(2,1)S(1)}, bf16[8,3,2,16,256]{4,3,2,1,0:T(8,128)(2,1)S(1)}, u32[]{:S(2)}, u32[]{:S(2)}) %collective-permute-start.10) | collective-permute-done | bytes 393248 | tf_op jit(solution)/shard_map/ppermute | solution.py:371
  39.6 2.2 %collective-permute-start.7 = (bf16[1,50,2,16,256]{4,3,2,1,0:T(8,128)(2,1)S(1)}, bf16[1,50,2,16,256]{4,3,2,1,0:T(8,128)(2,1)S(1)}, u32[]{:S(2)}, u32[]{:S(2)}) collective-permute-start(bf16[1,50,2,16,256]{4,3,2,1,0:T(8,128)(2,1)S(1)} %local_terms.7.rest_0_), channel_id=1, source_target_pairs={{0,16},{8,24},{16,0},{24,8},{1,17},{9,25},{17,1},{25,9},{2,18},{10... | collective-permute-start | bytes 2457608 | tf_op jit(solution)/shard_map/ppermute | solution.py:368
  41.7 6.3 %collective-permute-done.8.refs_1_ = bf16[8,3,2,16,256]{4,3,2,1,0:T(8,128)(2,1)S(1)} collective-permute-done((bf16[8,3,2,16,256]{4,3,2,1,0:T(8,128)(2,1)S(1)}, bf16[8,3,2,16,256]{4,3,2,1,0:T(8,128)(2,1)S(1)}, u32[]{:S(2)}, u32[]{:S(2)}) %collective-permute-start.8) | collective-permute-done | bytes 393248 | tf_op jit(solution)/shard_map/ppermute | solution.py:371
  48.0 2.0 %collective-permute-start.2 = (bf16[8,3,2,16,256]{4,3,2,1,0:T(8,128)(2,1)S(1)}, bf16[8,3,2,16,256]{4,3,2,1,0:T(8,128)(2,1)S(1)}, u32[]{:S(2)}, u32[]{:S(2)}) collective-permute-start(bf16[8,3,2,16,256]{4,3,2,1,0:T(8,128)(2,1)S(1)} %get-tuple-element.24.refs_3_), channel_id=1, source_target_pairs={{0,1},{1,0},{2,3},{3,2},{4,5},{5,4},{6,7},{7,6},{8,9},{9,8},{10,11... | collective-permute-start | bytes 1179656 | tf_op jit(solution)/shard_map/ppermute | solution.py:371
  50.0 6.4 %collective-permute-done.refs_1_ = bf16[8,3,2,16,256]{4,3,2,1,0:T(8,128)(2,1)S(1)} collective-permute-done((bf16[8,3,2,16,256]{4,3,2,1,0:T(8,128)(2,1)S(1)}, bf16[8,3,2,16,256]{4,3,2,1,0:T(8,128)(2,1)S(1)}, u32[]{:S(2)}, u32[]{:S(2)}) %collective-permute-start) | collective-permute-done | bytes 393248 | tf_op jit(solution)/shard_map/ppermute | solution.py:371
  56.4 2.1 %collective-permute-start.11 = (bf16[8,3,2,16,256]{4,3,2,1,0:T(8,128)(2,1)S(1)}, bf16[8,3,2,16,256]{4,3,2,1,0:T(8,128)(2,1)S(1)}, u32[]{:S(2)}, u32[]{:S(2)}) collective-permute-start(bf16[8,3,2,16,256]{4,3,2,1,0:T(8,128)(2,1)S(1)} %collective-permute-done.10.refs_4_), channel_id=1, source_target_pairs={{0,2},{1,7},{2,4},{3,1},{4,6},{5,3},{6,0},{7,5},{8,10},{9,15},{10,... | collective-permute-start | bytes 1179656 | tf_op jit(solution)/shard_map/ppermute | solution.py:371
  58.5 6.0 %collective-permute-done.2.refs_4_ = bf16[8,3,2,16,256]{4,3,2,1,0:T(8,128)(2,1)S(1)} collective-permute-done((bf16[8,3,2,16,256]{4,3,2,1,0:T(8,128)(2,1)S(1)}, bf16[8,3,2,16,256]{4,3,2,1,0:T(8,128)(2,1)S(1)}, u32[]{:S(2)}, u32[]{:S(2)}) %collective-permute-start.2) | collective-permute-done | bytes 393248 | tf_op jit(solution)/shard_map/ppermute | solution.py:371
  64.6 1.8 %collective-permute-start.9 = (bf16[8,3,2,16,256]{4,3,2,1,0:T(8,128)(2,1)S(1)}, bf16[8,3,2,16,256]{4,3,2,1,0:T(8,128)(2,1)S(1)}, u32[]{:S(2)}, u32[]{:S(2)}) collective-permute-start(bf16[8,3,2,16,256]{4,3,2,1,0:T(8,128)(2,1)S(1)} %collective-permute-done.8.refs_1_), channel_id=1, source_target_pairs={{0,2},{1,7},{2,4},{3,1},{4,6},{5,3},{6,0},{7,5},{8,10},{9,15},{10,... | collective-permute-start | bytes 1179656 | tf_op jit(solution)/shard_map/ppermute | solution.py:371
  66.4 2.4 %collective-permute-done.11.refs_5_ = bf16[8,3,2,16,256]{4,3,2,1,0:T(8,128)(2,1)S(1)} collective-permute-done((bf16[8,3,2,16,256]{4,3,2,1,0:T(8,128)(2,1)S(1)}, bf16[8,3,2,16,256]{4,3,2,1,0:T(8,128)(2,1)S(1)}, u32[]{:S(2)}, u32[]{:S(2)}) %collective-permute-start.11) | collective-permute-done | bytes 393248 | tf_op jit(solution)/shard_map/ppermute | solution.py:371
  68.8 0.0 collective-permute-start.1
  68.8 0.0 collective-permute-done.6.rest_1_
  68.8 1.3 %collective-permute-start.3 = (bf16[8,3,2,16,256]{4,3,2,1,0:T(8,128)(2,1)S(1)}, bf16[8,3,2,16,256]{4,3,2,1,0:T(8,128)(2,1)S(1)}, u32[]{:S(2)}, u32[]{:S(2)}) collective-permute-start(bf16[8,3,2,16,256]{4,3,2,1,0:T(8,128)(2,1)S(1)} %collective-permute-done.2.refs_4_), channel_id=1, source_target_pairs={{0,2},{1,7},{2,4},{3,1},{4,6},{5,3},{6,0},{7,5},{8,10},{9,15},{10,... | collective-permute-start | bytes 1179656 | tf_op jit(solution)/shard_map/ppermute | solution.py:371
  70.1 4.6 %local_terms.11.refs_6_ = bf16[2,50,2,16,256]{4,3,2,1,0:T(8,128)(2,1)S(1)} custom-call(s32[1]{0:T(128)} %bitcast.me_ref, bf16[256,512]{1,0:T(8,128)(2,1)S(1)} %get-tuple-element.25.mix_ref, bf16[256,256]{1,0:T(8,128)(2,1)S(1)} %get-tuple-element.26.dcol_ref, bf16[2,128,256]{2,1,0:T(8,128)(2,1)S(1)} %get-tuple-element.27.drow_ref, ...), custom_call_target="tpu_custom_call" | custom-call | flops 2415919104 | bytes 11010048 | tf_op jit(solution)/shard_map/local_terms/pallas_call | solution.py:251
  74.8 3.6 %collective-permute-done.9.refs_2_ = bf16[8,3,2,16,256]{4,3,2,1,0:T(8,128)(2,1)S(1)} collective-permute-done((bf16[8,3,2,16,256]{4,3,2,1,0:T(8,128)(2,1)S(1)}, bf16[8,3,2,16,256]{4,3,2,1,0:T(8,128)(2,1)S(1)}, u32[]{:S(2)}, u32[]{:S(2)}) %collective-permute-start.9) | collective-permute-done | bytes 393248 | tf_op jit(solution)/shard_map/ppermute | solution.py:371
  78.4 0.0 collective-permute-done.12.refs_7_
  78.4 0.9 depth_terms.3
  79.3 0.1 collective-permute-start.14
  79.4 1.8 %collective-permute-start.16 = (f32[2,4,256]{2,1,0:T(4,128)S(1)}, f32[2,4,256]{2,1,0:T(4,128)S(1)}, u32[]{:S(2)}, u32[]{:S(2)}) collective-permute-start(f32[2,4,256]{2,1,0:T(4,128)S(1)} %get-tuple-element.38), channel_id=1, source_target_pairs={{0,16},{8,24},{16,0},{24,8},{1,17},{9,25},{17,1},{25,9},{2,18},{10... | collective-permute-start | bytes 24584 | tf_op jit(solution)/shard_map/ppermute | solution.py:368
  81.2 5.7 %collective-permute-done.1.refs_2_ = bf16[8,3,2,16,256]{4,3,2,1,0:T(8,128)(2,1)S(1)} collective-permute-done((bf16[8,3,2,16,256]{4,3,2,1,0:T(8,128)(2,1)S(1)}, bf16[8,3,2,16,256]{4,3,2,1,0:T(8,128)(2,1)S(1)}, u32[]{:S(2)}, u32[]{:S(2)}) %collective-permute-start.1) | collective-permute-done | bytes 393248 | tf_op jit(solution)/shard_map/ppermute | solution.py:371
  86.8 0.0 collective-permute-start.18
  86.8 7.3 %collective-permute-done.3.refs_5_ = bf16[8,3,2,16,256]{4,3,2,1,0:T(8,128)(2,1)S(1)} collective-permute-done((bf16[8,3,2,16,256]{4,3,2,1,0:T(8,128)(2,1)S(1)}, bf16[8,3,2,16,256]{4,3,2,1,0:T(8,128)(2,1)S(1)}, u32[]{:S(2)}, u32[]{:S(2)}) %collective-permute-start.3) | collective-permute-done | bytes 393248 | tf_op jit(solution)/shard_map/ppermute | solution.py:371
  94.1 0.0 collective-permute-done.7.refs_7_
  94.1 0.9 depth_terms.2
  95.0 0.1 collective-permute-start.13
  95.1 1.4 %collective-permute-start.15 = (f32[2,4,256]{2,1,0:T(4,128)S(1)}, f32[2,4,256]{2,1,0:T(4,128)S(1)}, u32[]{:S(2)}, u32[]{:S(2)}) collective-permute-start(f32[2,4,256]{2,1,0:T(4,128)S(1)} %get-tuple-element.37), channel_id=1, source_target_pairs={{0,16},{8,24},{16,0},{24,8},{1,17},{9,25},{17,1},{25,9},{2,18},{10... | collective-permute-start | bytes 24584 | tf_op jit(solution)/shard_map/ppermute | solution.py:368
  96.5 0.0 collective-permute-done.14.refs_3_
  96.5 0.5 collective-permute-start.17
  97.0 0.0 collective-permute-done.16.refs_5_
  97.0 0.0 collective-permute-done.18.refs_7_
  97.0 0.0 collective-permute-done.13.refs_2_
  97.0 1.9 %collective-permute-done.15.refs_4_ = f32[2,4,256]{2,1,0:T(4,128)S(1)} collective-permute-done((f32[2,4,256]{2,1,0:T(4,128)S(1)}, f32[2,4,256]{2,1,0:T(4,128)S(1)}, u32[]{:S(2)}, u32[]{:S(2)}) %collective-permute-start.15) | collective-permute-done | bytes 8224 | tf_op jit(solution)/shard_map/ppermute | solution.py:368
  98.8 0.8 collective-permute-done.17.refs_6_
  99.6 0.6 join_columns.1
Async XLA Ops:
  3.7 4.6 %copy-start = (bf16[2,16,6,2,16,1024]{5,4,3,2,1,0:T(8,128)(2,1)S(1)}, bf16[2,16,6,2,16,1024]{5,4,3,2,1,0:T(8,128)(2,1)}, u32[]{:S(2)}) copy-start(bf16[2,16,6,2,16,1024]{5,4,3,2,1,0:T(8,128)(2,1)} %green_ref.11) | copy-start | bytes 37748740
  8.3 4.7 %copy-start.1 = (bf16[2,16,6,2,16,1024]{5,4,3,2,1,0:T(8,128)(2,1)S(1)}, bf16[2,16,6,2,16,1024]{5,4,3,2,1,0:T(8,128)(2,1)}, u32[]{:S(2)}) copy-start(bf16[2,16,6,2,16,1024]{5,4,3,2,1,0:T(8,128)(2,1)} %green_ref.11) | copy-start | bytes 37748740
  10.5 2.5 %collective-permute-start.4 = (bf16[1,50,2,16,256]{4,3,2,1,0:T(8,128)(2,1)S(1)}, bf16[1,50,2,16,256]{4,3,2,1,0:T(8,128)(2,1)S(1)}, u32[]{:S(2)}, u32[]{:S(2)}) collective-permute-start(bf16[1,50,2,16,256]{4,3,2,1,0:T(8,128)(2,1)S(1)} %local_terms.6.rest_0_), channel_id=1, source_target_pairs={{0,8},{8,0},{16,24},{24,16},{1,9},{9,1},{17,25},{25,17},{2,10},{10... | collective-permute-start | bytes 2457608 | tf_op jit(solution)/shard_map/ppermute | solution.py:368
  17.5 2.4 %collective-permute-start.5 = (bf16[1,50,2,16,256]{4,3,2,1,0:T(8,128)(2,1)S(1)}, bf16[1,50,2,16,256]{4,3,2,1,0:T(8,128)(2,1)S(1)}, u32[]{:S(2)}, u32[]{:S(2)}) collective-permute-start(bf16[1,50,2,16,256]{4,3,2,1,0:T(8,128)(2,1)S(1)} %local_terms.8.rest_0_), channel_id=1, source_target_pairs={{0,8},{8,0},{16,24},{24,16},{1,9},{9,1},{17,25},{25,17},{2,10},{10... | collective-permute-start | bytes 2457608 | tf_op jit(solution)/shard_map/ppermute | solution.py:368
  26.6 42.2 %collective-permute-start.6 = (bf16[2,50,2,16,256]{4,3,2,1,0:T(8,128)(2,1)S(1)}, bf16[2,50,2,16,256]{4,3,2,1,0:T(8,128)(2,1)S(1)}, u32[]{:S(2)}, u32[]{:S(2)}) collective-permute-start(bf16[2,50,2,16,256]{4,3,2,1,0:T(8,128)(2,1)S(1)} %local_terms.10.rest_0_), channel_id=1, source_target_pairs={{0,8},{8,0},{16,24},{24,16},{1,9},{9,1},{17,25},{25,17},{2,10},{10... | collective-permute-start | bytes 4915208 | tf_op jit(solution)/shard_map/ppermute | solution.py:368
  27.0 12.6 %collective-permute-start.10 = (bf16[8,3,2,16,256]{4,3,2,1,0:T(8,128)(2,1)S(1)}, bf16[8,3,2,16,256]{4,3,2,1,0:T(8,128)(2,1)S(1)}, u32[]{:S(2)}, u32[]{:S(2)}) collective-permute-start(bf16[8,3,2,16,256]{4,3,2,1,0:T(8,128)(2,1)S(1)} %get-tuple-element.33.refs_3_), channel_id=1, source_target_pairs={{0,1},{1,0},{2,3},{3,2},{4,5},{5,4},{6,7},{7,6},{8,9},{9,8},{10,11... | collective-permute-start | bytes 1179656 | tf_op jit(solution)/shard_map/ppermute | solution.py:371
  29.6 18.4 %collective-permute-start.8 = (bf16[8,3,2,16,256]{4,3,2,1,0:T(8,128)(2,1)S(1)}, bf16[8,3,2,16,256]{4,3,2,1,0:T(8,128)(2,1)S(1)}, u32[]{:S(2)}, u32[]{:S(2)}) collective-permute-start(bf16[8,3,2,16,256]{4,3,2,1,0:T(8,128)(2,1)S(1)} %get-tuple-element.32.refs_0_), channel_id=1, source_target_pairs={{0,1},{1,0},{2,3},{3,2},{4,5},{5,4},{6,7},{7,6},{8,9},{9,8},{10,11... | collective-permute-start | bytes 1179656 | tf_op jit(solution)/shard_map/ppermute | solution.py:371
  29.7 26.8 %collective-permute-start = (bf16[8,3,2,16,256]{4,3,2,1,0:T(8,128)(2,1)S(1)}, bf16[8,3,2,16,256]{4,3,2,1,0:T(8,128)(2,1)S(1)}, u32[]{:S(2)}, u32[]{:S(2)}) collective-permute-start(bf16[8,3,2,16,256]{4,3,2,1,0:T(8,128)(2,1)S(1)} %get-tuple-element.23.rest_0_.refs_0_), channel_id=1, source_target_pairs={{0,1},{1,0},{2,3},{3,2},{4,5},{5,4},{6,7},{7,6},{8,9},{9,8},{10,11... | collective-permute-start | bytes 1179656 | tf_op jit(solution)/shard_map/ppermute | solution.py:371
  31.6 46.8 %collective-permute-start.12 = (bf16[1,50,2,16,256]{4,3,2,1,0:T(8,128)(2,1)S(1)}, bf16[1,50,2,16,256]{4,3,2,1,0:T(8,128)(2,1)S(1)}, u32[]{:S(2)}, u32[]{:S(2)}) collective-permute-start(bf16[1,50,2,16,256]{4,3,2,1,0:T(8,128)(2,1)S(1)} %local_terms.9.rest_0_), channel_id=1, source_target_pairs={{0,16},{8,24},{16,0},{24,8},{1,17},{9,25},{17,1},{25,9},{2,18},{10... | collective-permute-start | bytes 2457608 | tf_op jit(solution)/shard_map/ppermute | solution.py:368
  39.6 54.6 %collective-permute-start.7 = (bf16[1,50,2,16,256]{4,3,2,1,0:T(8,128)(2,1)S(1)}, bf16[1,50,2,16,256]{4,3,2,1,0:T(8,128)(2,1)S(1)}, u32[]{:S(2)}, u32[]{:S(2)}) collective-permute-start(bf16[1,50,2,16,256]{4,3,2,1,0:T(8,128)(2,1)S(1)} %local_terms.7.rest_0_), channel_id=1, source_target_pairs={{0,16},{8,24},{16,0},{24,8},{1,17},{9,25},{17,1},{25,9},{2,18},{10... | collective-permute-start | bytes 2457608 | tf_op jit(solution)/shard_map/ppermute | solution.py:368
  48.0 16.6 %collective-permute-start.2 = (bf16[8,3,2,16,256]{4,3,2,1,0:T(8,128)(2,1)S(1)}, bf16[8,3,2,16,256]{4,3,2,1,0:T(8,128)(2,1)S(1)}, u32[]{:S(2)}, u32[]{:S(2)}) collective-permute-start(bf16[8,3,2,16,256]{4,3,2,1,0:T(8,128)(2,1)S(1)} %get-tuple-element.24.refs_3_), channel_id=1, source_target_pairs={{0,1},{1,0},{2,3},{3,2},{4,5},{5,4},{6,7},{7,6},{8,9},{9,8},{10,11... | collective-permute-start | bytes 1179656 | tf_op jit(solution)/shard_map/ppermute | solution.py:371
  56.4 12.4 %collective-permute-start.11 = (bf16[8,3,2,16,256]{4,3,2,1,0:T(8,128)(2,1)S(1)}, bf16[8,3,2,16,256]{4,3,2,1,0:T(8,128)(2,1)S(1)}, u32[]{:S(2)}, u32[]{:S(2)}) collective-permute-start(bf16[8,3,2,16,256]{4,3,2,1,0:T(8,128)(2,1)S(1)} %collective-permute-done.10.refs_4_), channel_id=1, source_target_pairs={{0,2},{1,7},{2,4},{3,1},{4,6},{5,3},{6,0},{7,5},{8,10},{9,15},{10,... | collective-permute-start | bytes 1179656 | tf_op jit(solution)/shard_map/ppermute | solution.py:371
  64.6 13.8 %collective-permute-start.9 = (bf16[8,3,2,16,256]{4,3,2,1,0:T(8,128)(2,1)S(1)}, bf16[8,3,2,16,256]{4,3,2,1,0:T(8,128)(2,1)S(1)}, u32[]{:S(2)}, u32[]{:S(2)}) collective-permute-start(bf16[8,3,2,16,256]{4,3,2,1,0:T(8,128)(2,1)S(1)} %collective-permute-done.8.refs_1_), channel_id=1, source_target_pairs={{0,2},{1,7},{2,4},{3,1},{4,6},{5,3},{6,0},{7,5},{8,10},{9,15},{10,... | collective-permute-start | bytes 1179656 | tf_op jit(solution)/shard_map/ppermute | solution.py:371
  68.8 18.0 %collective-permute-start.1 = (bf16[8,3,2,16,256]{4,3,2,1,0:T(8,128)(2,1)S(1)}, bf16[8,3,2,16,256]{4,3,2,1,0:T(8,128)(2,1)S(1)}, u32[]{:S(2)}, u32[]{:S(2)}) collective-permute-start(bf16[8,3,2,16,256]{4,3,2,1,0:T(8,128)(2,1)S(1)} %collective-permute-done.refs_1_), channel_id=1, source_target_pairs={{0,2},{1,7},{2,4},{3,1},{4,6},{5,3},{6,0},{7,5},{8,10},{9,15},{10,... | collective-permute-start | bytes 1179656 | tf_op jit(solution)/shard_map/ppermute | solution.py:371
  68.8 25.3 %collective-permute-start.3 = (bf16[8,3,2,16,256]{4,3,2,1,0:T(8,128)(2,1)S(1)}, bf16[8,3,2,16,256]{4,3,2,1,0:T(8,128)(2,1)S(1)}, u32[]{:S(2)}, u32[]{:S(2)}) collective-permute-start(bf16[8,3,2,16,256]{4,3,2,1,0:T(8,128)(2,1)S(1)} %collective-permute-done.2.refs_4_), channel_id=1, source_target_pairs={{0,2},{1,7},{2,4},{3,1},{4,6},{5,3},{6,0},{7,5},{8,10},{9,15},{10,... | collective-permute-start | bytes 1179656 | tf_op jit(solution)/shard_map/ppermute | solution.py:371
  79.3 17.2 %collective-permute-start.14 = (f32[2,4,256]{2,1,0:T(4,128)S(1)}, f32[2,4,256]{2,1,0:T(4,128)S(1)}, u32[]{:S(2)}, u32[]{:S(2)}) collective-permute-start(f32[2,4,256]{2,1,0:T(4,128)S(1)} %get-tuple-element.36), channel_id=1, source_target_pairs={{0,8},{8,0},{16,24},{24,16},{1,9},{9,1},{17,25},{25,17},{2,10},{10... | collective-permute-start | bytes 24584 | tf_op jit(solution)/shard_map/ppermute | solution.py:368
  79.4 17.6 %collective-permute-start.16 = (f32[2,4,256]{2,1,0:T(4,128)S(1)}, f32[2,4,256]{2,1,0:T(4,128)S(1)}, u32[]{:S(2)}, u32[]{:S(2)}) collective-permute-start(f32[2,4,256]{2,1,0:T(4,128)S(1)} %get-tuple-element.38), channel_id=1, source_target_pairs={{0,16},{8,24},{16,0},{24,8},{1,17},{9,25},{17,1},{25,9},{2,18},{10... | collective-permute-start | bytes 24584 | tf_op jit(solution)/shard_map/ppermute | solution.py:368
  86.8 10.2 %collective-permute-start.18 = (f32[2,4,256]{2,1,0:T(4,128)S(1)}, f32[2,4,256]{2,1,0:T(4,128)S(1)}, u32[]{:S(2)}, u32[]{:S(2)}) collective-permute-start(f32[2,4,256]{2,1,0:T(4,128)S(1)} %get-tuple-element.40), channel_id=1, source_target_pairs={{0,24},{8,16},{16,8},{24,0},{1,25},{9,17},{17,9},{25,1},{2,26},{10... | collective-permute-start | bytes 24584 | tf_op jit(solution)/shard_map/ppermute | solution.py:368
  95.0 1.9 %collective-permute-start.13 = (f32[2,4,256]{2,1,0:T(4,128)S(1)}, f32[2,4,256]{2,1,0:T(4,128)S(1)}, u32[]{:S(2)}, u32[]{:S(2)}) collective-permute-start(f32[2,4,256]{2,1,0:T(4,128)S(1)} %get-tuple-element.35), channel_id=1, source_target_pairs={{0,8},{8,0},{16,24},{24,16},{1,9},{9,1},{17,25},{25,17},{2,10},{10... | collective-permute-start | bytes 24584 | tf_op jit(solution)/shard_map/ppermute | solution.py:368
  95.1 3.7 %collective-permute-start.15 = (f32[2,4,256]{2,1,0:T(4,128)S(1)}, f32[2,4,256]{2,1,0:T(4,128)S(1)}, u32[]{:S(2)}, u32[]{:S(2)}) collective-permute-start(f32[2,4,256]{2,1,0:T(4,128)S(1)} %get-tuple-element.37), channel_id=1, source_target_pairs={{0,16},{8,24},{16,0},{24,8},{1,17},{9,25},{17,1},{25,9},{2,18},{10... | collective-permute-start | bytes 24584 | tf_op jit(solution)/shard_map/ppermute | solution.py:368
  96.5 3.1 %collective-permute-start.17 = (f32[2,4,256]{2,1,0:T(4,128)S(1)}, f32[2,4,256]{2,1,0:T(4,128)S(1)}, u32[]{:S(2)}, u32[]{:S(2)}) collective-permute-start(f32[2,4,256]{2,1,0:T(4,128)S(1)} %get-tuple-element.39), channel_id=1, source_target_pairs={{0,24},{8,16},{16,8},{24,0},{1,25},{9,17},{17,9},{25,1},{2,26},{10... | collective-permute-start | bytes 24584 | tf_op jit(solution)/shard_map/ppermute | solution.py:368
